TPU v7x, 128 devices: a whole 4x4x4 slice. The times are simulated.
128 devices in a mesh: ctx: 32 (over x, y, core), head: 4 (over z).
Axes of the slice: x: 4, y: 4, z: 4, core: 2. Of those that a mesh axis runs over, the one named last changes fastest.
Arguments:
- tokens: bfloat16 [8192, 2048], P('ctx'), may hold values from -6 to 6
- qkv_weight: bfloat16 [2048, 3, 16, 128], P(None, None, 'head'), may hold values from -0.125 to 0.125
- small_weight: bfloat16 [2048, 16, 15], P(None, 'head'), may hold values from -0.125 to 0.125
- head_param: float32 [16, 2], P('head'), as said below
- norm_gain: float32 [128], replicated, may hold values from 0.1 to 1.9
- out_weight: bfloat16 [16, 128, 2048], P('head'), may hold values from -0.125 to 0.125
- grad_out: bfloat16 [8192, 2048], P('ctx'), may hold values from -6 to 6
Outputs:
- layer_out: bfloat16 [8192, 2048], P('ctx', 'head')
- grad_tokens: bfloat16 [8192, 2048], P('ctx', 'head')
Inputs may be any that keep to these rules, and one draw needn't show every extreme that they name: `head_param`: column 0 holds each head's decay rate, positive; column 1 a bias added before the write strength's sigmoid.
All inputs are finite; a program needn't handle non-finite values.
Results may differ from a plain program's by a relative error of at most 0.017.
Values may be sent and summed in bfloat16 or wider, within the bound.
A program may use at most 128 MiB of HBM per device.

v0:
```python
import jax
import jax.numpy as jnp
from jax import lax
from jax.sharding import PartitionSpec as P

BLOCK = 64


def swapped(array, axis, stride):
    return lax.ppermute(array, axis, [(i, i ^ 1 << stride) for i in range(lax.axis_size(axis))])


def for_sending(array):

    def short(part):
        return part.astype(jnp.bfloat16) if part.dtype == jnp.float32 else part

    return jax.tree.map(short, array)


def mat_mul(left, right):
    return jnp.matmul(left, right, precision=lax.Precision.HIGHEST)


def flip_last(array_in):
    return jnp.swapaxes(array_in, -1, -2)


def unit_scale(values):
    return values * lax.rsqrt(jnp.sum(values * values, -1, keepdims=True) + 1e-06)


def block_pieces(q_in, k_in, v_in, beta_w, decay_log):
    length = q_in.shape[-2]
    cum_log = jnp.cumsum(decay_log, axis=-1)
    row_id = lax.broadcasted_iota(jnp.int32, (length, length), 0)
    col_id = lax.broadcasted_iota(jnp.int32, (length, length), 1)
    inclusive = row_id >= col_id
    strict = row_id > col_id
    spread = cum_log[..., :, None] - cum_log[..., None, :]
    decay_mat = jnp.where(inclusive, jnp.exp(jnp.where(inclusive, spread, 0.0)), 0.0)
    key_gram = mat_mul(k_in, flip_last(k_in))
    lower_part = jnp.where(strict, beta_w[..., :, None] * decay_mat * key_gram, 0.0)
    system = lower_part + jnp.eye(length, dtype=jnp.float32)
    growth = jnp.exp(cum_log)
    right_side = jnp.concatenate(
        [beta_w[..., None] * v_in, (beta_w * growth)[..., None] * k_in], -1
    )
    solved = jax.scipy.linalg.solve_triangular(system, right_side, lower=True, unit_diagonal=True)
    value_dim = v_in.shape[-1]
    new_values = solved[..., :value_dim]
    key_mix = solved[..., value_dim:]
    scores = mat_mul(q_in, flip_last(k_in)) * decay_mat
    intra_out = mat_mul(scores, new_values)
    query_mix = growth[..., None] * q_in - mat_mul(scores, key_mix)
    tail_decay = jnp.exp(cum_log[..., -1:] - cum_log)
    tail_keys = tail_decay[..., None] * k_in
    eye_key = jnp.eye(k_in.shape[-1], dtype=jnp.float32)
    transit = jnp.exp(cum_log[..., -1])[..., None, None] * eye_key - mat_mul(
        flip_last(key_mix), tail_keys
    )
    own_state = mat_mul(flip_last(new_values), tail_keys)
    return (intra_out, query_mix, transit, own_state)


def butterfly(transit, own_state):
    total_count = transit.shape[0]
    eye_key = jnp.eye(transit.shape[-1], dtype=jnp.float32)
    prefix = jnp.broadcast_to(eye_key, transit.shape)
    block_a = transit
    block_u = own_state
    found_all = []
    block_len = 1
    while block_len < total_count:
        pair_count = total_count // (2 * block_len)
        split_a = block_a.reshape((pair_count, 2) + block_a.shape[1:])
        split_u = block_u.reshape((pair_count, 2) + block_u.shape[1:])
        split_p = prefix.reshape((pair_count, 2, block_len) + prefix.shape[1:])
        low_a = split_a[:, 0]
        high_a = split_a[:, 1]
        low_u = split_u[:, 0]
        high_u = split_u[:, 1]
        upper_p = split_p[:, 1]
        arriving = mat_mul(low_u[:, None], upper_p)
        moved_p = mat_mul(low_a[:, None], upper_p)
        found_all.append(
            jnp.stack([jnp.zeros_like(arriving), arriving], 1).reshape(own_state.shape)
        )
        prefix = jnp.stack([split_p[:, 0], moved_p], 1).reshape(prefix.shape)
        block_a = mat_mul(low_a, high_a)
        block_u = mat_mul(low_u, high_a) + high_u
        block_len = block_len * 2
    return (found_all, prefix, block_a[0], block_u[0])


def merge_step(pair_now, prefix, pair_peer, is_upper):
    a_now = pair_now[0]
    u_now = pair_now[1]
    a_peer = pair_peer[0]
    u_peer = pair_peer[1]
    arriving = jnp.where(is_upper, mat_mul(u_peer, prefix), 0.0)
    new_prefix = jnp.where(is_upper, mat_mul(a_peer, prefix), prefix)
    new_a = jnp.where(is_upper, mat_mul(a_peer, a_now), mat_mul(a_now, a_peer))
    new_u = jnp.where(is_upper, mat_mul(u_peer, a_now) + u_now, mat_mul(u_now, a_peer) + u_peer)
    return (arriving, new_prefix, jnp.stack([new_a, new_u], 0))


def on_device(tokens, qkv_weight, small_weight, head_param, norm_gain, out_weight, grad_out):
    row_count = tokens.shape[0]
    model_width = tokens.shape[1]
    head_count = qkv_weight.shape[2]
    head_dim = qkv_weight.shape[3]
    extra_cols = small_weight.shape[2]
    levels_n = extra_cols - 2
    block_count = row_count // BLOCK
    index_ctx = lax.axis_index("ctx")
    shard_bits = lax.axis_size("ctx").bit_length() - 1
    local_bits = block_count.bit_length() - 1
    flat_qkv = qkv_weight.reshape(model_width, 3 * head_count * head_dim)
    flat_small = small_weight.reshape(model_width, head_count * extra_cols)
    flat_out = out_weight.reshape(head_count * head_dim, model_width)
    proj = jnp.dot(tokens, flat_qkv, preferred_element_type=jnp.float32).reshape(
        row_count, 3, head_count, head_dim
    )
    gate_pre = jnp.dot(tokens, flat_small, preferred_element_type=jnp.float32).reshape(
        row_count, head_count, extra_cols
    )

    def to_blocks(tensor):
        return jnp.swapaxes(tensor.reshape((block_count, BLOCK) + tensor.shape[1:]), 1, 2)

    def section_local(q_raw, k_raw, v_raw, gate_in):
        gate_blk = to_blocks(gate_in)
        beta_w = jax.nn.sigmoid(gate_blk[..., levels_n + 1] + head_param[:, 1][None, :, None])
        decay_log = -head_param[:, 0][None, :, None] * jax.nn.sigmoid(gate_blk[..., levels_n])
        weights = jax.nn.softplus(gate_blk[..., :levels_n])
        intra_out, query_mix, transit, own_state = block_pieces(
            to_blocks(unit_scale(q_raw)),
            to_blocks(unit_scale(k_raw)),
            to_blocks(v_raw),
            beta_w,
            decay_log,
        )
        found_all, prefix, block_a, block_u = butterfly(transit, own_state)
        local_out = weights[..., 0:1] * intra_out
        for level_no in range(len(found_all)):
            local_out = local_out + weights[..., level_no + 1 : level_no + 2] * mat_mul(
                query_mix, flip_last(found_all[level_no])
            )
        query_hat = mat_mul(query_mix, flip_last(prefix))
        far_weights = weights[..., local_bits + 1 : local_bits + 1 + shard_bits]
        return (jnp.stack([block_a, block_u], 0), (local_out, query_hat, far_weights))

    def section_out(local_out, query_hat, far_weights, incoming):
        summed = local_out
        for level_no in range(len(incoming)):
            summed = summed + far_weights[..., level_no : level_no + 1] * mat_mul(
                query_hat, flip_last(incoming[level_no])[None]
            )
        return summed * lax.rsqrt(jnp.mean(summed * summed, -1, keepdims=True) + 1e-06) * norm_gain

    (summary, carried), pull_local = jax.vjp(
        section_local, proj[:, 0], proj[:, 1], proj[:, 2], gate_pre
    )
    pair_now = summary
    prefix = jnp.broadcast_to(jnp.eye(head_dim, dtype=jnp.float32), summary.shape[1:])
    saved_steps = []
    incoming = []
    for bit_no in range(shard_bits):
        pair_peer = swapped(pair_now.astype(jnp.bfloat16), "ctx", bit_no).astype(pair_now.dtype)
        is_upper = index_ctx // 2**bit_no % 2 == 1
        saved_steps.append((pair_now, prefix, is_upper))
        arriving, prefix, pair_now = merge_step(pair_now, prefix, pair_peer, is_upper)
        incoming.append(arriving)
    incoming = tuple(incoming)
    normed, pull_out = jax.vjp(section_out, carried[0], carried[1], carried[2], incoming)
    normed_low = (
        jnp.swapaxes(normed, 1, 2)
        .reshape((row_count,) + normed.shape[1:2] + normed.shape[3:])
        .reshape(row_count, head_count * head_dim)
        .astype(jnp.bfloat16)
    )
    out_part = jnp.dot(normed_low, flat_out, preferred_element_type=jnp.float32)
    layer_out = lax.psum_scatter(
        out_part.astype(jnp.bfloat16), "head", scatter_dimension=1, tiled=True
    )
    grad_normed = jnp.dot(grad_out, flat_out.T, preferred_element_type=jnp.float32)
    grad_normed = to_blocks(grad_normed.reshape(row_count, head_count, head_dim))
    grad_local, grad_hat, grad_far, grad_incoming = pull_out(grad_normed)
    grad_pair = jnp.zeros_like(summary)
    grad_prefix = jnp.zeros(summary.shape[1:], jnp.float32)
    for bit_no in reversed(range(shard_bits)):
        pair_now, prefix, is_upper = saved_steps[bit_no]
        grad_arrived = grad_incoming[bit_no]
        through_prefix = jnp.stack(
            [mat_mul(grad_prefix, flip_last(prefix)), mat_mul(grad_arrived, flip_last(prefix))], 0
        )
        through_prefix = jnp.where(is_upper, through_prefix, 0.0)
        pair_peer, peer_grad, peer_through = (
            swapped(pair_now.astype(jnp.bfloat16), "ctx", bit_no).astype(pair_now.dtype),
            swapped(for_sending(grad_pair), "ctx", bit_no).astype(grad_pair.dtype),
            swapped(for_sending(through_prefix), "ctx", bit_no).astype(through_prefix.dtype),
        )

        def step_local(pair_in, prefix_in, peer_in):
            return merge_step(pair_in, prefix_in, peer_in, is_upper)

        step_out, pull_step = jax.vjp(step_local, pair_now, prefix, pair_peer)
        own_part, grad_prefix, unused_peer = pull_step(
            (grad_arrived, grad_prefix, grad_pair + peer_grad)
        )
        grad_pair = own_part + peer_through
    grad_q, grad_k, grad_v, grad_gate = pull_local((grad_pair, (grad_local, grad_hat, grad_far)))
    grad_proj = (
        jnp.stack([grad_q, grad_k, grad_v], 1)
        .astype(jnp.bfloat16)
        .reshape(row_count, 3 * head_count * head_dim)
    )
    grad_small = grad_gate.astype(jnp.bfloat16).reshape(row_count, head_count * extra_cols)
    grad_part = jnp.dot(grad_proj, flat_qkv.T, preferred_element_type=jnp.float32)
    grad_part = grad_part + jnp.dot(grad_small, flat_small.T, preferred_element_type=jnp.float32)
    grad_tokens = lax.psum_scatter(
        grad_part.astype(jnp.bfloat16), "head", scatter_dimension=1, tiled=True
    )
    return (layer_out, grad_tokens)


def solution(mesh):
    placed = (
        P("ctx", None),
        P(None, None, "head", None),
        P(None, "head", None),
        P("head", None),
        P(),
        P("head", None, None),
        P("ctx", None),
    )
    return jax.shard_map(
        on_device,
        mesh=mesh,
        in_specs=placed,
        out_specs=(P("ctx", "head"), P("ctx", "head")),
        check_vma=False,
    )
```

profile of v0, /device:TPU:1, one launch (start us, length us, event | category | flops | bytes accessed | tf_op | source)
XLA Modules:
  0.0 469.2 jit_solution(10189610739382682199)
XLA Ops:
  7.2 11.1 %reshape.431 = bf16[2048,1536]{1,0:T(8,128)(2,1)} reshape(bf16[2048,3,4,128]{3,2,1,0:T(4,128)(2,1)} %param.8) | data formatting | bytes 12582912 | tf_op jit(solution)/shard_map/reshape | solution.py:119
  18.4 8.7 %copy.495 = bf16[1536,2048]{1,0:T(8,128)(2,1)} copy(bf16[1536,2048]{0,1:T(8,128)(2,1)} %bitcast.930) | data formatting | bytes 12582912 | tf_op jit(solution)/shard_map/dot_general | solution.py:122
  27.0 4.3 fusion.60
  56.7 80.4 %custom-call.10 = f32[4,4,1,64,64]{3,4,2,1,0:T(8,128)} custom-call(f32[4,4,1,64,64]{4,3,2,1,0:T(8,128)} %add_bitcast_fusion.1), custom_call_target="InvertDiagBlocksLowerTriangular" | custom-call | tf_op jit(solution)/shard_map/jvp(jit(_solve_triangular))/vmap(vmap())/triangular_solve | solution.py:49
  149.4 3.0 collective-permute-start.5
  158.8 3.2 compare_select_fusion.2
  178.7 3.0 fusion.480
  232.3 3.0 collective-permute-start.2
  236.5 4.1 collective-permute-done.2
  243.5 4.3 collective-permute-done.3
  252.6 3.2 collective-permute-done.4
  256.9 3.1 fusion.87
  285.2 3.0 fusion.109
  290.1 4.6 fusion.97
  307.9 4.0 collective-permute-start.14
  329.4 5.0 %fusion.15 = f32[4,4,64,13]{1,0,2,3:T(4,128)} fusion(f32[4,4,64,1]{1,0,2,3:T(4,128)S(1)} %bitcast.972, f32[4,4,64,1]{1,0,2,3:T(4,128)} %bitcast.973, f32[4,4,64,1]{1,0,2,3:T(4,128)} %bitcast.974, f32[4,4,64,5]{1,0,2,3:T(4,128)S(1)} %pad_add_fusion.5, f32[4,4,64,15]{1,0,2,3:T(4,128)} %bitcast.940), kind=kLoop, calls=%fused_computation.15 | loop fusion | flops 199680 | bytes 139264 | tf_op jit(solution)/shard_map/transpose(jvp(jit(softplus)))/mul | solution.py:136
  339.2 6.5 %collective-permute-done.7 = bf16[2,4,128,128]{3,2,1,0:T(8,128)(2,1)S(1)} collective-permute-done((bf16[2,4,128,128]{3,2,1,0:T(8,128)(2,1)S(1)}, bf16[2,4,128,128]{3,2,1,0:T(8,128)(2,1)S(1)}, u32[]{:S(2)}, u32[]{:S(2)}) %collective-permute-start.7) | collective-permute-done | bytes 262176 | tf_op jit(solution)/shard_map/ppermute | solution.py:10
  351.3 5.8 %collective-permute-done.9 = bf16[2,4,128,128]{3,2,1,0:T(8,128)(2,1)S(1)} collective-permute-done((bf16[2,4,128,128]{3,2,1,0:T(8,128)(2,1)S(1)}, bf16[2,4,128,128]{3,2,1,0:T(8,128)(2,1)S(1)}, u32[]{:S(2)}, u32[]{:S(2)}) %collective-permute-start.9) | collective-permute-done | bytes 262176 | tf_op jit(solution)/shard_map/ppermute | solution.py:10
  361.9 4.0 collective-permute-done.11
  369.4 4.0 collective-permute-start.13
  410.9 4.8 %reduce_window_sum.26 = f32[4,4,64,1]{3,2,1,0:T(8,128)S(1)} reduce-window(f32[4,4,64,1]{3,2,1,0:T(8,128)S(1)} %copy.642, f32[]{:T(128)} %constant.147.clone.1), window={size=1x1x64x1 pad=0_0x0_0x0_63x0_0}, to_apply=%region_23.24 | reduce-window | flops 64512 | bytes 8196 | tf_op jit(solution)/shard_map/transpose(jvp(jit(cumsum)))/reduce_window_sum | solution.py:35
  418.9 3.1 fusion.62
  435.1 5.8 %fusion.8 = bf16[256,2048]{1,0:T(8,128)(2,1)} fusion(f32[256,2048]{1,0:T(8,128)S(1)} %convolution_bitcast_fusion, bf16[2048,3,4,128]{3,2,1,0:T(4,128)(2,1)} %param.8, bf16[256,1,4,128]{3,0,2,1:T(8,128)(2,1)S(1)} %bitcast.980, bf16[256,1,4,128]{3,0,2,1:T(8,128)(2,1)S(1)} %get-tuple-element.56, bf16[256,1,4,128]{3,0,2,1:T(8,128)(2,1)S(1)} %get-tuple-element.55), kind=kOutput, calls=%fused_computation.9 | convolution fusion | flops 1612447744 | bytes 10223616 | tf_op jit(solution)/shard_map/dot_general | solution.py:220
  440.9 21.3 %reduce-scatter.5.cloned.1.call-done = bf16[256,512]{1,0:T(8,128)(2,1)} async-done(((bf16[256,2048]{1,0:T(8,128)(2,1)}), bf16[256,512]{1,0:T(8,128)(2,1)}) %reduce-scatter.5.cloned.1.call-update) | async-done | bytes 262160 | tf_op jit(solution)/shard_map/reduce_scatter | solution.py:222
  (604 shorter events, 248.5 us)
Async XLA Ops:
  7.2 249.5 %copy-start = (bf16[4,128,2048]{2,1,0:T(8,128)(2,1)S(1)}, bf16[4,128,2048]{2,1,0:T(8,128)(2,1)}, u32[]{:S(2)}) copy-start(bf16[4,128,2048]{2,1,0:T(8,128)(2,1)} %param.12) | copy-start | bytes 6291460
  7.2 433.7 %reduce-scatter.3.cloned.1.call-start = ((), (), s32[]{:S(2)}) async-start(), calls=%async_computation.2 | async-start | bytes 1310720 | tf_op jit(solution)/shard_map/reduce_scatter | solution.py:184
  33.4 138.9 %copy-start.24 = (f32[256,1,4,128]{3,0,2,1:T(8,128)}, f32[256,1,4,128]{3,0,2,1:T(8,128)S(1)}, u32[]{:S(2)}) copy-start(f32[256,1,4,128]{3,0,2,1:T(8,128)S(1)} %get-tuple-element.57) | copy-start | bytes 1572868
  51.8 85.4 %copy-start.140 = (f32[4,4]{1,0:T(4,128)S(1)}, f32[4,4]{1,0:T(4,128)}, u32[]{:S(2)}) copy-start(f32[4,4]{1,0:T(4,128)} %slice_bitcast_fusion.116) | copy-start | bytes 196
  52.5 87.2 %copy-start.104 = (pred[64,64]{1,0:T(8,128)(4,1)}, pred[64,64]{1,0:T(8,128)(4,1)S(1)}, u32[]{:S(2)}) copy-start(pred[64,64]{1,0:T(8,128)(4,1)S(1)} %iota_compare_fusion.4) | copy-start | bytes 12292
  147.3 74.9 %collective-permute-start = (bf16[2,4,128,128]{3,2,1,0:T(8,128)(2,1)}, bf16[2,4,128,128]{3,2,1,0:T(8,128)(2,1)S(1)}, u32[]{:S(2)}, u32[]{:S(2)}) collective-permute-start(bf16[2,4,128,128]{3,2,1,0:T(8,128)(2,1)} %pad_maximum_fusion.1), channel_id=1, source_target_pairs={{0,4},{4,0},{8,12},{12,8},{16,20},{20,16},{24,28},{28,24},{32,36},... | collective-permute-start | bytes 786440 | tf_op jit(solution)/shard_map/ppermute | solution.py:10
  149.4 77.9 %collective-permute-start.5 = (bf16[2,4,128,128]{3,2,1,0:T(8,128)(2,1)}, bf16[2,4,128,128]{3,2,1,0:T(8,128)(2,1)}, u32[]{:S(2)}, u32[]{:S(2)}) collective-permute-start(bf16[2,4,128,128]{3,2,1,0:T(8,128)(2,1)} %broadcast_in_dim.213), channel_id=1, source_target_pairs={{0,64},{4,68},{8,72},{12,76},{16,80},{20,84},{24,88},{28,92},{32,9... | collective-permute-start | bytes 786440 | tf_op jit(solution)/shard_map/ppermute | solution.py:10
  222.2 38.4 %copy-start.13 = (f32[4,4,64,128]{3,2,1,0:T(8,128)}, f32[4,4,64,128]{3,2,1,0:T(8,128)S(1)}, u32[]{:S(2)}) copy-start(f32[4,4,64,128]{3,2,1,0:T(8,128)S(1)} %fusion.176) | copy-start | bytes 1572868
  223.5 7.7 %collective-permute-start.1 = (bf16[2,4,128,128]{3,2,1,0:T(8,128)(2,1)S(1)}, bf16[2,4,128,128]{3,2,1,0:T(8,128)(2,1)S(1)}, u32[]{:S(2)}, u32[]{:S(2)}) collective-permute-start(bf16[2,4,128,128]{3,2,1,0:T(8,128)(2,1)S(1)} %pad_maximum_fusion.2), channel_id=1, source_target_pairs={{0,8},{4,12},{8,0},{12,4},{16,24},{20,28},{24,16},{28,20},{32,40},... | collective-permute-start | bytes 786440 | tf_op jit(solution)/shard_map/ppermute | solution.py:10
  229.7 30.9 %copy-start.14 = (f32[4,4,64,128]{3,2,0,1:T(8,128)}, f32[4,4,64,128]{3,2,0,1:T(8,128)S(1)}, u32[]{:S(2)}) copy-start(f32[4,4,64,128]{3,2,0,1:T(8,128)S(1)} %fusion.239) | copy-start | bytes 1572868
  232.3 8.3 %collective-permute-start.2 = (bf16[2,4,128,128]{3,2,1,0:T(8,128)(2,1)S(1)}, bf16[2,4,128,128]{3,2,1,0:T(8,128)(2,1)S(1)}, u32[]{:S(2)}, u32[]{:S(2)}) collective-permute-start(bf16[2,4,128,128]{3,2,1,0:T(8,128)(2,1)S(1)} %pad_maximum_fusion.3), channel_id=1, source_target_pairs={{0,16},{4,20},{8,24},{12,28},{16,0},{20,4},{24,8},{28,12},{32,48},... | collective-permute-start | bytes 786440 | tf_op jit(solution)/shard_map/ppermute | solution.py:10
  241.8 6.0 %collective-permute-start.3 = (bf16[2,4,128,128]{3,2,1,0:T(8,128)(2,1)S(1)}, bf16[2,4,128,128]{3,2,1,0:T(8,128)(2,1)S(1)}, u32[]{:S(2)}, u32[]{:S(2)}) collective-permute-start(bf16[2,4,128,128]{3,2,1,0:T(8,128)(2,1)S(1)} %pad_maximum_fusion.4), channel_id=1, source_target_pairs={{0,32},{4,36},{8,40},{12,44},{16,48},{20,52},{24,56},{28,60},{32,0... | collective-permute-start | bytes 786440 | tf_op jit(solution)/shard_map/ppermute | solution.py:10
  249.0 6.8 %collective-permute-start.4 = (bf16[2,4,128,128]{3,2,1,0:T(8,128)(2,1)S(1)}, bf16[2,4,128,128]{3,2,1,0:T(8,128)(2,1)S(1)}, u32[]{:S(2)}, u32[]{:S(2)}) collective-permute-start(bf16[2,4,128,128]{3,2,1,0:T(8,128)(2,1)S(1)} %pad_maximum_fusion.5), channel_id=1, source_target_pairs={{0,64},{4,68},{8,72},{12,76},{16,80},{20,84},{24,88},{28,92},{32,9... | collective-permute-start | bytes 786440 | tf_op jit(solution)/shard_map/ppermute | solution.py:10
  290.1 172.1 %reduce-scatter.5.cloned.1.call-start = ((), (), s32[]{:S(2)}) async-start(), calls=%async_computation.3 | async-start | bytes 1310720 | tf_op jit(solution)/shard_map/reduce_scatter | solution.py:222
  307.9 69.3 %collective-permute-start.14 = (bf16[2,4,128,128]{3,2,1,0:T(8,128)(2,1)}, bf16[2,4,128,128]{3,2,1,0:T(8,128)(2,1)}, u32[]{:S(2)}, u32[]{:S(2)}) collective-permute-start(bf16[2,4,128,128]{3,2,1,0:T(8,128)(2,1)} %fusion.77), channel_id=1, source_target_pairs={{0,4},{4,0},{8,12},{12,8},{16,20},{20,16},{24,28},{28,24},{32,36},... | collective-permute-start | bytes 786440 | tf_op jit(solution)/shard_map/ppermute | solution.py:10
  312.7 55.7 %collective-permute-start.12 = (bf16[2,4,128,128]{3,2,1,0:T(8,128)(2,1)}, bf16[2,4,128,128]{3,2,1,0:T(8,128)(2,1)}, u32[]{:S(2)}, u32[]{:S(2)}) collective-permute-start(bf16[2,4,128,128]{3,2,1,0:T(8,128)(2,1)} %fusion.76), channel_id=1, source_target_pairs={{0,8},{4,12},{8,0},{12,4},{16,24},{20,28},{24,16},{28,20},{32,40},... | collective-permute-start | bytes 786440 | tf_op jit(solution)/shard_map/ppermute | solution.py:10
  314.7 44.9 %collective-permute-start.10 = (bf16[2,4,128,128]{3,2,1,0:T(8,128)(2,1)}, bf16[2,4,128,128]{3,2,1,0:T(8,128)(2,1)}, u32[]{:S(2)}, u32[]{:S(2)}) collective-permute-start(bf16[2,4,128,128]{3,2,1,0:T(8,128)(2,1)} %fusion.75), channel_id=1, source_target_pairs={{0,16},{4,20},{8,24},{12,28},{16,0},{20,4},{24,8},{28,12},{32,48},... | collective-permute-start | bytes 786440 | tf_op jit(solution)/shard_map/ppermute | solution.py:10
  318.1 30.1 %collective-permute-start.8 = (bf16[2,4,128,128]{3,2,1,0:T(8,128)(2,1)}, bf16[2,4,128,128]{3,2,1,0:T(8,128)(2,1)}, u32[]{:S(2)}, u32[]{:S(2)}) collective-permute-start(bf16[2,4,128,128]{3,2,1,0:T(8,128)(2,1)} %fusion.74), channel_id=1, source_target_pairs={{0,32},{4,36},{8,40},{12,44},{16,48},{20,52},{24,56},{28,60},{32,0... | collective-permute-start | bytes 786440 | tf_op jit(solution)/shard_map/ppermute | solution.py:10
  319.2 18.6 %collective-permute-start.6 = (bf16[2,4,128,128]{3,2,1,0:T(8,128)(2,1)}, bf16[2,4,128,128]{3,2,1,0:T(8,128)(2,1)}, u32[]{:S(2)}, u32[]{:S(2)}) collective-permute-start(bf16[2,4,128,128]{3,2,1,0:T(8,128)(2,1)} %fusion.73), channel_id=1, source_target_pairs={{0,64},{4,68},{8,72},{12,76},{16,80},{20,84},{24,88},{28,92},{32,9... | collective-permute-start | bytes 786440 | tf_op jit(solution)/shard_map/ppermute | solution.py:10
  338.9 6.8 %collective-permute-start.7 = (bf16[2,4,128,128]{3,2,1,0:T(8,128)(2,1)S(1)}, bf16[2,4,128,128]{3,2,1,0:T(8,128)(2,1)S(1)}, u32[]{:S(2)}, u32[]{:S(2)}) collective-permute-start(bf16[2,4,128,128]{3,2,1,0:T(8,128)(2,1)S(1)} %fusion.183), channel_id=1, source_target_pairs={{0,32},{4,36},{8,40},{12,44},{16,48},{20,52},{24,56},{28,60},{32,0... | collective-permute-start | bytes 786440 | tf_op jit(solution)/shard_map/ppermute | solution.py:10
  349.2 7.9 %collective-permute-start.9 = (bf16[2,4,128,128]{3,2,1,0:T(8,128)(2,1)S(1)}, bf16[2,4,128,128]{3,2,1,0:T(8,128)(2,1)S(1)}, u32[]{:S(2)}, u32[]{:S(2)}) collective-permute-start(bf16[2,4,128,128]{3,2,1,0:T(8,128)(2,1)S(1)} %fusion.184), channel_id=1, source_target_pairs={{0,16},{4,20},{8,24},{12,28},{16,0},{20,4},{24,8},{28,12},{32,48},... | collective-permute-start | bytes 786440 | tf_op jit(solution)/shard_map/ppermute | solution.py:10
  360.6 5.3 %collective-permute-start.11 = (bf16[2,4,128,128]{3,2,1,0:T(8,128)(2,1)S(1)}, bf16[2,4,128,128]{3,2,1,0:T(8,128)(2,1)S(1)}, u32[]{:S(2)}, u32[]{:S(2)}) collective-permute-start(bf16[2,4,128,128]{3,2,1,0:T(8,128)(2,1)S(1)} %fusion.185), channel_id=1, source_target_pairs={{0,8},{4,12},{8,0},{12,4},{16,24},{20,28},{24,16},{28,20},{32,40},... | collective-permute-start | bytes 786440 | tf_op jit(solution)/shard_map/ppermute | solution.py:10
  369.4 5.2 %collective-permute-start.13 = (bf16[2,4,128,128]{3,2,1,0:T(8,128)(2,1)S(1)}, bf16[2,4,128,128]{3,2,1,0:T(8,128)(2,1)S(1)}, u32[]{:S(2)}, u32[]{:S(2)}) collective-permute-start(bf16[2,4,128,128]{3,2,1,0:T(8,128)(2,1)S(1)} %fusion.186), channel_id=1, source_target_pairs={{0,4},{4,0},{8,12},{12,8},{16,20},{20,16},{24,28},{28,24},{32,36},... | collective-permute-start | bytes 786440 | tf_op jit(solution)/shard_map/ppermute | solution.py:10
  435.0 27.1 %copy-start.1 = (bf16[4,128,2048]{2,1,0:T(8,128)(2,1)S(1)}, bf16[4,128,2048]{2,1,0:T(8,128)(2,1)}, u32[]{:S(2)}) copy-start(bf16[4,128,2048]{2,1,0:T(8,128)(2,1)} %param.12) | copy-start | bytes 6291460
  (141 other events, 613.1 us)
Sparse Core Ops, SparseCore 0:
  290.2 26.3 reduce-scatter.2
  441.0 21.1 reduce-scatter.4
where the time goes:
time: 477 us; the launch traced here: 469 us
  other arithmetic  144 us (30%)
  matrix products  139 us (29%)
  local copies, waits for them, and re-layouts  93.3 us (20%)
  waiting for transfers between devices  50.9 us (11%)
  starting transfers between devices  25.4 us (5%)
  between operations  17.4 us (4%)
    dot_general x127, matrix products, mat_mul(): return jnp.matmul(left, right, precision=lax.Precision.HIGHEST)  115 us
    another operation x5, other arithmetic, block_pieces(): jax.scipy.linalg.solve_triangular(system, right_side, lower=True, unit_di...  83.9 us
    ppermute x15, waiting for transfers between devices, swapped(): lax.ppermute(array, axis, [(i, i ^ 1 << stride) for i in range(lax.axis_s...  29.6 us
    ppermute x15, starting transfers between devices, swapped(): lax.ppermute(array, axis, [(i, i ^ 1 << stride) for i in range(lax.axis_s...  25.3 us
    mul x15, local copies, waits for them, and re-layouts, section_out(): far_weights[..., level_no:level_no + 1]  23.9 us
    reduce_scatter x1, waiting for transfers between devices, on_device(): lax.psum_scatter(grad_part.astype(jnp.bfloat16), 'head', scatter_dimensio...  21.3 us
    reshape x1, local copies, waits for them, and re-layouts, on_device(): flat_qkv = qkv_weight.reshape(model_width, 3 * head_count * head_dim)  11.1 us
  transfers between devices with their start and end apart: 17, of which 9 were waited for; matrix products, arithmetic and copies ran while one was open for 42% of the time, Pallas kernels for 0%

commit v1 on v0

v1 whole, which is shorter than its diff:
```python
import functools

import jax
import jax.numpy as jnp
from jax import lax
from jax.experimental import pallas as pl
from jax.experimental.pallas import tpu as pltpu
from jax.sharding import PartitionSpec as P

BF = jnp.bfloat16
F32 = jnp.float32
LANES = 32
VM = pltpu.VMEM


def nn(a, b):
    return lax.dot_general(a, b, (((1,), (0,)), ((), ())), preferred_element_type=F32)


def nt(a, b):
    return lax.dot_general(a, b, (((1,), (1,)), ((), ())), preferred_element_type=F32)


def tn(a, b):
    return lax.dot_general(a, b, (((0,), (0,)), ((), ())), preferred_element_type=F32)


def sigmoid(x):
    return 1.0 / (1.0 + jnp.exp(-x))


def softplus(x):
    return jnp.maximum(x, 0.0) + jnp.log(1.0 + jnp.exp(-jnp.abs(x)))


def iotas(n, m):
    return lax.broadcasted_iota(jnp.int32, (n, m), 0), lax.broadcasted_iota(jnp.int32, (n, m), 1)


def col(array, lane):
    return array[:, lane : lane + 1]


def head_rows(param_ref, heads, rows):
    lane = lax.broadcasted_iota(jnp.int32, (rows, heads * LANES), 1)
    rate = jnp.zeros((rows, heads * LANES), F32)
    bias = jnp.zeros((rows, heads * LANES), F32)
    for h in range(heads):
        here = lane // LANES == h
        rate = jnp.where(here, param_ref[h, 0], rate)
        bias = jnp.where(here, param_ref[h, 1], bias)
    return rate, bias


def proj_kernel(heads, extra, tok_ref, w_ref, sw_ref, proj_ref, gate_ref, wflat_ref, swflat_ref, wide, swide):
    step = pl.program_id(0)
    parts = 3 * heads
    depth = tok_ref.shape[1]
    wide[...] = w_ref[...].astype(F32)
    swide[...] = sw_ref[...].astype(F32)
    for part in range(parts):
        wflat_ref[:, part * 128 : (part + 1) * 128] = wide[pl.ds(part, depth, stride=parts), :].astype(BF)
    swflat_ref[...] = jnp.zeros_like(swflat_ref)
    for h in range(heads):
        swflat_ref[:, h * LANES : h * LANES + extra] = swide[pl.ds(h, depth, stride=heads), :].astype(BF)

    @pl.when(step == 0)
    def _():
        proj_ref[...] = jnp.zeros_like(proj_ref)
        gate_ref[...] = jnp.zeros_like(gate_ref)

    tok = tok_ref[...]
    proj_ref[...] += nn(tok, wflat_ref[...])
    gate_ref[...] += nn(tok, swflat_ref[...])


def project(tokens, qkv_weight, small_weight):
    rows, width = tokens.shape
    heads = qkv_weight.shape[2]
    extra = small_weight.shape[2]
    parts = 3 * heads
    depth = 256
    return pl.pallas_call(
        functools.partial(proj_kernel, heads, extra),
        grid=(width // depth,),
        in_specs=[
            pl.BlockSpec((rows, depth), lambda i: (0, i)),
            pl.BlockSpec((depth * parts, 128), lambda i: (i, 0)),
            pl.BlockSpec((depth * heads, extra), lambda i: (i, 0)),
        ],
        out_specs=[
            pl.BlockSpec((rows, parts * 128), lambda i: (0, 0)),
            pl.BlockSpec((rows, heads * LANES), lambda i: (0, 0)),
            pl.BlockSpec((depth, parts * 128), lambda i: (i, 0)),
            pl.BlockSpec((depth, heads * LANES), lambda i: (i, 0)),
        ],
        out_shape=[
            jax.ShapeDtypeStruct((rows, parts * 128), F32),
            jax.ShapeDtypeStruct((rows, heads * LANES), F32),
            jax.ShapeDtypeStruct((width, parts * 128), BF),
            jax.ShapeDtypeStruct((width, heads * LANES), BF),
        ],
        scratch_shapes=[VM((depth * parts, 128), F32), VM((depth * heads, extra), F32)],
        name="project",
    )(tokens, qkv_weight.reshape(width * parts, 128), small_weight.reshape(width * heads, extra))


def unit(values):
    scale = lax.rsqrt(jnp.sum(values * values, -1, keepdims=True) + 1e-06)
    return values * scale, scale


def running_log(gate, rate, n):
    row, lane = iotas(n, n)
    lower = jnp.where(row >= lane, 1.0, 0.0).astype(F32)
    return lax.dot_general(
        lower, -rate * sigmoid(gate), (((1,), (0,)), ((), ())),
        precision=lax.Precision.HIGHEST, preferred_element_type=F32,
    )


def mask_rows(n, masks):
    row, lane = iotas(n, n)
    cross = jnp.bitwise_xor(row, lane)
    for k in range(masks.shape[0]):
        masks[k] = jnp.where(jnp.right_shift(cross, k) == 1, 1.0, 0.0).astype(BF)


def local_kernel(heads, levels, group, param_ref, proj_ref, gate_ref, au_ref, e_ref, s_ref, lp_ref, t_ref, m_ref,
                 nk_ref, core_ref, qh_ref, clog_ref, masks, low):
    n = proj_ref.shape[0]
    gate = gate_ref[...]
    rate, bias = head_rows(param_ref, heads, n)
    clog = running_log(gate, rate, n)
    clog_ref[...] = clog
    clog_t = clog.T
    beta_all = sigmoid(gate + bias)
    lam_all = softplus(gate)
    mask_rows(n, masks)
    row, lane = iotas(n, n)
    cross = jnp.bitwise_xor(row, lane)
    incl = row >= lane
    strict = row > lane
    half = n // 2
    for first in range(0, heads, group):
        hs = range(first, first + group)
        keep = {}
        tb = {}
        for h in hs:
            base = h * LANES
            q, _ = unit(proj_ref[:, h * 128 : (h + 1) * 128])
            k, _ = unit(proj_ref[:, (heads + h) * 128 : (heads + h + 1) * 128])
            v = proj_ref[:, (2 * heads + h) * 128 : (2 * heads + h + 1) * 128]
            qb, kb = q.astype(BF), k.astype(BF)
            beta = col(beta_all, base + levels + 1)
            cc = col(clog, base + levels)
            end = clog_t[base + levels : base + levels + 1, n - 1 : n]
            crow = clog_t[base + levels : base + levels + 1, :]
            e = jnp.where(incl, jnp.exp(cc - crow), 0.0)
            s = (nt(qb, kb) * e).astype(BF)
            lp = jnp.where(strict, nt(kb, kb) * e, 0.0)
            lo = (lp * beta).astype(BF)
            e_ref[h] = e.astype(BF)
            s_ref[h] = s
            lp_ref[h] = lp.astype(BF)
            low[h % group] = lo
            tb[h] = jnp.where(row == lane, 1.0, 0.0).astype(BF) - lo * masks[0]
            grow = jnp.exp(cc)
            keep[h] = (grow * q, (v * beta).astype(BF), ((beta * grow) * k).astype(BF),
                       (jnp.exp(end - cc) * k).astype(BF), end)
        for level in range(1, masks.shape[0]):
            for h in hs:
                w = nn(low[h % group] * masks[level], tb[h]).astype(BF)
                tb[h] = tb[h] - nn(tb[h], w).astype(BF)
        for h in hs:
            base = h * LANES
            gq, vb, kbg, tk, end = keep[h]
            t_ref[h] = tb[h]
            m = nn(s_ref[h], tb[h])
            mb = m.astype(BF)
            m_ref[h] = mb
            mix = nn(tb[h], jnp.concatenate([vb, kbg], 1)).astype(BF)
            nk_ref[h] = mix
            au = tn(mix, tk)
            r2, l2 = iotas(128, 128)
            au_ref[h, 0:128] = au[0:128].astype(BF)
            au_ref[h, 128:256] = (jnp.where(r2 == l2, jnp.exp(end), 0.0) - au[128:256]).astype(BF)
            lam = jnp.where(cross < 64, col(lam_all, base),
                            jnp.where(cross < 128, col(lam_all, base + 1), col(lam_all, base + 2)))
            core_ref[h] = nn((m * lam).astype(BF), vb)
            qh_ref[h] = (gq - nn(mb, kbg)).astype(BF)


def local_forward(head_param, proj, gate, levels):
    rows = proj.shape[0]
    heads = head_param.shape[0]
    group = 2
    square = jax.ShapeDtypeStruct((heads, rows, rows), BF)
    bits = rows.bit_length() - 1
    return pl.pallas_call(
        functools.partial(local_kernel, heads, levels, group),
        in_specs=[pl.BlockSpec(memory_space=pltpu.SMEM), pl.BlockSpec(memory_space=VM), pl.BlockSpec(memory_space=VM)],
        out_specs=[pl.BlockSpec(memory_space=VM)] * 10,
        out_shape=[
            jax.ShapeDtypeStruct((heads, 256, 128), BF),
            square, square, square, square, square,
            jax.ShapeDtypeStruct((heads, rows, 256), BF),
            jax.ShapeDtypeStruct((heads, rows, 128), F32),
            jax.ShapeDtypeStruct((heads, rows, 128), BF),
            jax.ShapeDtypeStruct((rows, heads * LANES), F32),
        ],
        scratch_shapes=[VM((bits, rows, rows), BF), VM((group, rows, rows), BF)],
        name="local_forward",
    )(head_param, proj, gate)


def out_kernel(heads, levels, far, near, gate_ref, core_ref, qh_ref, x_ref, gain_ref, gout_ref, ow_ref,
               part_ref, g_ref, dqh_ref, gx_ref, dlam_ref):
    n = gate_ref.shape[0]
    lam_all = softplus(gate_ref[...])
    lane = lax.broadcasted_iota(jnp.int32, (n, heads * LANES), 1)
    gain = gain_ref[...]
    dlam = jnp.zeros((n, heads * LANES), F32)
    grad_normed = nt(gout_ref[...], ow_ref[...])
    normed = []
    for h in range(heads):
        base = h * LANES
        qh = qh_ref[h]
        x = x_ref[h]
        w = nt(qh, x)
        core = core_ref[h]
        fw = [col(lam_all, base + near + j) for j in range(far)]
        for j in range(far):
            core = core + fw[j] * w[:, j * 128 : (j + 1) * 128]
        rs = lax.rsqrt(jnp.mean(core * core, -1, keepdims=True) + 1e-06)
        unit_core = core * rs
        normed.append((unit_core * gain).astype(BF))
        gy = grad_normed[:, h * 128 : (h + 1) * 128] * gain
        g = rs * (gy - unit_core * jnp.mean(gy * unit_core, -1, keepdims=True))
        g_ref[h] = g.astype(BF)
        fg = jnp.concatenate([(fw[j] * g).astype(BF) for j in range(far)], 1)
        for j in range(far):
            here = jnp.sum(g * w[:, j * 128 : (j + 1) * 128], -1, keepdims=True)
            dlam = jnp.where(lane == base + near + j, here, dlam)
        dqh_ref[h] = nn(fg, x).astype(BF)
        gx_ref[h] = tn(fg, qh).astype(BF)
    dlam_ref[...] = dlam
    part_ref[...] = nn(jnp.concatenate(normed, 1), ow_ref[...]).astype(BF)


def out_stage(gate, core, qh, x, gain, grad_out, out_weight, levels, far, near):
    rows, width = grad_out.shape
    heads = core.shape[0]
    return pl.pallas_call(
        functools.partial(out_kernel, heads, levels, far, near),
        in_specs=[pl.BlockSpec(memory_space=VM)] * 7,
        out_specs=[pl.BlockSpec(memory_space=VM)] * 5,
        out_shape=[
            jax.ShapeDtypeStruct((rows, width), BF),
            jax.ShapeDtypeStruct((heads, rows, 128), BF),
            jax.ShapeDtypeStruct((heads, rows, 128), BF),
            jax.ShapeDtypeStruct((heads, far * 128, 128), BF),
            jax.ShapeDtypeStruct((rows, heads * LANES), F32),
        ],
        name="out_stage",
    )(gate, core, qh, x, gain, grad_out, out_weight)


def back_kernel(heads, levels, group, param_ref, proj_ref, gate_ref, clog_ref, e_ref, s_ref, lp_ref, t_ref, m_ref,
                nk_ref, g_ref, dqh_ref, dau_ref, dlam_ref, wflat_ref, swflat_ref, part_ref):
    n = proj_ref.shape[0]
    gate = gate_ref[...]
    rate, bias = head_rows(param_ref, heads, n)
    clog = clog_ref[...]
    beta_all = sigmoid(gate + bias)
    sig_all = sigmoid(gate)
    lam_all = softplus(gate)
    row, lane = iotas(n, n)
    cross = jnp.bitwise_xor(row, lane)
    strict = row > lane
    wide = lax.broadcasted_iota(jnp.int32, (n, heads * LANES), 1)
    dlam = dlam_ref[...]
    dlog = jnp.zeros((n, heads * LANES), F32)
    dbeta_all = jnp.zeros((n, heads * LANES), F32)
    last = lax.broadcasted_iota(jnp.int32, (n, 1), 0) == n - 1
    out = [None] * (3 * heads)
    for first in range(0, heads, group):
        for h in range(first, first + group):
            base = h * LANES
            q, rq = unit(proj_ref[:, h * 128 : (h + 1) * 128])
            k, rk = unit(proj_ref[:, (heads + h) * 128 : (heads + h + 1) * 128])
            v = proj_ref[:, (2 * heads + h) * 128 : (2 * heads + h + 1) * 128]
            qb, kb = q.astype(BF), k.astype(BF)
            beta = col(beta_all, base + levels + 1)
            cc = col(clog, base + levels)
            end = clog[n - 1 : n, base + levels : base + levels + 1]
            grow = jnp.exp(cc)
            tail = jnp.exp(end - cc)
            vb = (v * beta).astype(BF)
            kbg = ((beta * grow) * k).astype(BF)
            tk = (tail * k).astype(BF)
            g, dqh = g_ref[h], dqh_ref[h]
            mb, tb, mix = m_ref[h], t_ref[h], nk_ref[h]
            m = mb.astype(F32)
            lam = jnp.where(cross < 64, col(lam_all, base),
                            jnp.where(cross < 128, col(lam_all, base + 1), col(lam_all, base + 2)))
            dmw = nt(g, vb)
            prod = m * dmw
            zero = jnp.zeros_like(prod)
            for j, pick in enumerate((cross < 64, (cross >= 64) & (cross < 128), cross >= 128)):
                here = jnp.sum(jnp.where(pick, prod, zero), -1, keepdims=True)
                dlam = jnp.where(wide == base + j, here, dlam)
            mw = (m * lam).astype(BF)
            dm = (lam * dmw - nt(dqh, kbg)).astype(BF)
            dau = dau_ref[h]
            du, da = dau[0:128], dau[128:256]
            dnv = nt(tk, du)
            dkt = -nt(tk, da)
            dtk = nn(mix[:, 0:128], du) - nn(mix[:, 128:256], da)
            dmix = jnp.concatenate([dnv.astype(BF), dkt.astype(BF)], 1)
            back = tn(tb, dmix)
            dvb2, dkbg2 = back[:, 0:128], back[:, 128:256]
            dst = nt(dm, tb)
            dstb = dst.astype(BF)
            dvb = tn(mw, g) + dvb2
            both = tn(mb, jnp.concatenate([dqh, dstb], 1))
            dkbg = dkbg2 - both[:, 0:128]
            dlow = both[:, 128:] + nt(back.astype(BF), mix)
            dlow = jnp.where(strict, -dlow, 0.0)
            e = e_ref[h].astype(F32)
            dp = (dst * e).astype(BF)
            lp = lp_ref[h].astype(F32)
            dbeta = jnp.sum(dlow * lp, -1, keepdims=True)
            dkk = (dlow * (beta * e)).astype(BF)
            dq1 = nn(dp, kb)
            dk1 = tn(dp, qb)
            dk2 = nn(dkk, kb)
            dk3 = tn(dkk, kb)
            qr, kr = qb.astype(F32), kb.astype(F32)
            dqf, dtf, dkf = dqh.astype(F32), dtk, dkbg
            gq = jnp.sum(dqf * q, -1, keepdims=True)
            kk = jnp.sum(dkf * k, -1, keepdims=True)
            dtail = jnp.sum(dtf * k, -1, keepdims=True) * tail
            dc = jnp.sum(qr * dq1 + kr * (dk2 - dk1 - dk3), -1, keepdims=True)
            dc = dc + grow * (gq + beta * kk) - dtail
            r2, l2 = iotas(128, 128)
            trace = jnp.sum(jnp.where(r2 == l2, da.astype(F32), 0.0), keepdims=True)
            dend = jnp.sum(dtail, keepdims=True) + jnp.exp(end) * trace
            dc = dc + jnp.where(last, dend, 0.0)
            dbeta = dbeta + jnp.sum(dvb * v, -1, keepdims=True) + grow * kk
            dq = dq1 + grow * dqf
            dk = dk1 + dk2 + dk3 + (beta * grow) * dkf + tail * dtf
            dv = beta * dvb
            out[h] = (rq * (dq - q * jnp.sum(q * dq, -1, keepdims=True))).astype(BF)
            out[heads + h] = (rk * (dk - k * jnp.sum(k * dk, -1, keepdims=True))).astype(BF)
            out[2 * heads + h] = dv.astype(BF)
            dlog = jnp.where(wide == base + levels, dc, dlog)
            dbeta_all = jnp.where(wide == base + levels + 1, dbeta, dbeta_all)
    upper = jnp.where(lane >= row, 1.0, 0.0).astype(F32)
    dstep = lax.dot_general(upper, dlog, (((1,), (0,)), ((), ())),
                            precision=lax.Precision.HIGHEST, preferred_element_type=F32)
    dgate = dlam * sig_all - rate * sig_all * (1.0 - sig_all) * dstep + beta_all * (1.0 - beta_all) * dbeta_all
    dgate = dgate.astype(BF)
    dproj = jnp.concatenate(out, 1)
    width = part_ref.shape[1]
    for j in range(0, width, 512):
        part = nt(dproj, wflat_ref[j : j + 512, :]) + nt(dgate, swflat_ref[j : j + 512, :])
        part_ref[:, j : j + 512] = part.astype(BF)


def back_stage(head_param, proj, gate, clog, saved, g, dqh, dau, dlam, wflat, swflat, levels):
    rows = proj.shape[0]
    heads = head_param.shape[0]
    return pl.pallas_call(
        functools.partial(back_kernel, heads, levels, 1),
        in_specs=[pl.BlockSpec(memory_space=pltpu.SMEM)] + [pl.BlockSpec(memory_space=VM)] * 15,
        out_specs=pl.BlockSpec(memory_space=VM),
        out_shape=jax.ShapeDtypeStruct((rows, wflat.shape[0]), BF),
        compiler_params=pltpu.CompilerParams(vmem_limit_bytes=60 * 2**20),
        name="back_stage",
    )(head_param, proj, gate, clog, *saved, g, dqh, dau, dlam, wflat, swflat)


def swapped(array, axis, stride):
    return lax.ppermute(array, axis, [(i, i ^ 1 << stride) for i in range(lax.axis_size(axis))])


def mat_mul(left, right):
    return jnp.matmul(left, right)


def flip_last(array_in):
    return jnp.swapaxes(array_in, -1, -2)


def merge_step(pair_now, prefix, pair_peer, is_upper):
    a_now = pair_now[0]
    u_now = pair_now[1]
    a_peer = pair_peer[0]
    u_peer = pair_peer[1]
    arriving = jnp.where(is_upper, mat_mul(u_peer, prefix), 0.0)
    new_prefix = jnp.where(is_upper, mat_mul(a_peer, prefix), prefix)
    new_a = jnp.where(is_upper, mat_mul(a_peer, a_now), mat_mul(a_now, a_peer))
    new_u = jnp.where(is_upper, mat_mul(u_peer, a_now) + u_now, mat_mul(u_now, a_peer) + u_peer)
    return (arriving, new_prefix, jnp.stack([new_a, new_u], 0))


def on_device(tokens, qkv_weight, small_weight, head_param, norm_gain, out_weight, grad_out):
    rows, width = tokens.shape
    heads = qkv_weight.shape[2]
    levels = small_weight.shape[2] - 2
    near = (rows // 64).bit_length()
    far = lax.axis_size("ctx").bit_length() - 1
    index_ctx = lax.axis_index("ctx")
    proj, gate, wflat, swflat = project(tokens, qkv_weight, small_weight)
    au, *saved, core, qh, clog = local_forward(head_param, proj, gate, levels)
    au = au.astype(F32)
    pair_now = jnp.stack([au[:, 128:], au[:, :128]], 0)
    prefix = jnp.broadcast_to(jnp.eye(128, dtype=jnp.float32), (heads, 128, 128))
    saved_steps = []
    incoming = []
    for bit_no in range(far):
        pair_peer = swapped(pair_now.astype(BF), "ctx", bit_no).astype(F32)
        is_upper = index_ctx // 2**bit_no % 2 == 1
        saved_steps.append((pair_now, prefix, is_upper))
        arriving, prefix, pair_now = merge_step(pair_now, prefix, pair_peer, is_upper)
        incoming.append(arriving)
    x = jnp.concatenate(incoming, 1).astype(BF)
    out_part, g, dqh, gx, dlam = out_stage(
        gate, core, qh, x, norm_gain.reshape(1, -1), grad_out, out_weight.reshape(heads * 128, width),
        levels, far, near)
    layer_out = lax.psum_scatter(out_part, "head", scatter_dimension=1, tiled=True)
    gx = gx.astype(F32)
    grad_incoming = [gx[:, i * 128 : (i + 1) * 128] for i in range(far)]
    grad_pair = jnp.zeros_like(pair_now)
    grad_prefix = jnp.zeros(prefix.shape, F32)
    for bit_no in reversed(range(far)):
        pair_now, prefix, is_upper = saved_steps[bit_no]
        grad_arrived = grad_incoming[bit_no]
        through = jnp.stack(
            [mat_mul(grad_prefix, flip_last(prefix)), mat_mul(grad_arrived, flip_last(prefix))], 0)
        through = jnp.where(is_upper, through, 0.0)
        pair_peer, peer_grad, peer_through = (
            swapped(pair_now.astype(BF), "ctx", bit_no).astype(F32),
            swapped(grad_pair.astype(BF), "ctx", bit_no).astype(F32),
            swapped(through.astype(BF), "ctx", bit_no).astype(F32),
        )

        def step_local(pair_in, prefix_in, peer_in):
            return merge_step(pair_in, prefix_in, peer_in, is_upper)

        step_out, pull_step = jax.vjp(step_local, pair_now, prefix, pair_peer)
        own_part, grad_prefix, unused_peer = pull_step((grad_arrived, grad_prefix, grad_pair + peer_grad))
        grad_pair = own_part + peer_through
    dau = jnp.concatenate([grad_pair[1], grad_pair[0]], 1).astype(BF)
    grad_part = back_stage(head_param, proj, gate, clog, saved, g, dqh, dau, dlam, wflat, swflat, levels)
    grad_tokens = lax.psum_scatter(grad_part, "head", scatter_dimension=1, tiled=True)
    return (layer_out, grad_tokens)


def solution(mesh):
    placed = (
        P("ctx", None),
        P(None, None, "head", None),
        P(None, "head", None),
        P("head", None),
        P(),
        P("head", None, None),
        P("ctx", None),
    )
    return jax.shard_map(
        on_device,
        mesh=mesh,
        in_specs=placed,
        out_specs=(P("ctx", "head"), P("ctx", "head")),
        check_vma=False,
    )
```

time: 477 us -> 180 us (0.38); the launches traced: 469 us -> 179 us
  other arithmetic: 144 us -> 1.91 us
  matrix products: 139 us -> 16.5 us
  local copies, waits for them, and re-layouts: 93.3 us -> 6.55 us
  Pallas kernels: 0 us -> 44.1 us
  waiting for transfers between devices: 50.9 us -> 67.3 us
    dot_general x134 -> x62, matrix products: 133 us -> 16.5 us  [mat_mul(): return jnp.matmul(left, right)]
    another operation x10 -> x2, other arithmetic: 92.5 us -> 0.1 us  [the longest x5 83.9 us: block_pieces(): jax.scipy.linalg.solve_triangular(system, right_side, lower=True, unit_di...]
    pallas_call x0 -> x4, Pallas kernels: none -> 44.1 us  [the longest x1 15.2 us: back_stage(): pl.pallas_call(functools.partial(back_kernel, heads, levels, 1), in_specs...]
    mul x29 -> x0, local copies, waits for them, and re-layouts: 40.1 us -> none  [the longest x15 23.9 us: section_out(): far_weights[..., level_no:level_no + 1]]
    ppermute x15, waiting for transfers between devices: 29.6 us -> 46.4 us  [swapped(): lax.ppermute(array, axis, [(i, i ^ 1 << stride) for i in range(lax.axis_s...]
    convert_element_type x14 -> x11, other arithmetic: 16.4 us -> 0.58 us  [the longest x5 0.27 us: on_device(): through.astype(BF)]
    reshape x3 -> x0, local copies, waits for them, and re-layouts: 14.8 us -> none  [the longest x1 11.1 us: on_device(): flat_qkv = qkv_weight.reshape(model_width, 3 * head_count * head_dim)]
    mul x9 -> x0, other arithmetic: 13.6 us -> none  [the longest x1 5.01 us: section_local(): weights = jax.nn.softplus(gate_blk[..., :levels_n])]
  transfers between devices with their start and end apart: 17 -> 17, of which waited for: 9 -> 14; matrix products, arithmetic and copies ran while one was open for 42% -> 7% of each run, Pallas kernels for 0% -> 8%
where the time goes in v1:
time: 180 us; the launch traced here: 179 us
  waiting for transfers between devices  67.3 us (37%)
  Pallas kernels  44.1 us (24%)
  starting transfers between devices  27.5 us (15%)
  matrix products  16.5 us (9%)
  between operations  14.8 us (8%)
  local copies, waits for them, and re-layouts  6.55 us (4%)
  other arithmetic  1.91 us (1%)
    ppermute x15, waiting for transfers between devices, swapped(): lax.ppermute(array, axis, [(i, i ^ 1 << stride) for i in range(lax.axis_s...  46.4 us
    ppermute x15, starting transfers between devices, swapped(): lax.ppermute(array, axis, [(i, i ^ 1 << stride) for i in range(lax.axis_s...  27.4 us
    reduce_scatter x1, waiting for transfers between devices, on_device(): lax.psum_scatter(grad_part, 'head', scatter_dimension=1, tiled=True)  20.9 us
    dot_general x62, matrix products, mat_mul(): return jnp.matmul(left, right)  16.5 us
    pallas_call x1, Pallas kernels, back_stage(): pl.pallas_call(functools.partial(back_kernel, heads, levels, 1), in_specs...  15.2 us
    pallas_call x1, Pallas kernels, local_forward(): pl.pallas_call(functools.partial(local_kernel, heads, levels, group), in_...  11 us
    pallas_call x1, Pallas kernels, project(): pl.pallas_call(functools.partial(proj_kernel, heads, extra), grid=(width...  10.7 us
    pallas_call x1, Pallas kernels, out_stage(): pl.pallas_call(functools.partial(out_kernel, heads, levels, far, near), i...  7.31 us
  transfers between devices with their start and end apart: 17, of which 14 were waited for; matrix products, arithmetic and copies ran while one was open for 7% of the time, Pallas kernels for 8%

profile of v1, /device:TPU:1, one launch (start us, length us, event | category | flops | bytes accessed | tf_op | source)
XLA Modules:
  0.0 178.7 jit_solution(9501692055318135691)
XLA Ops:
  7.2 3.9 %copy.9 = bf16[2048,4,15]{2,1,0:T(4,128)(2,1)} copy(bf16[2048,4,15]{0,1,2:T(4,128)(2,1)} %param.9) | data formatting | bytes 491520 | tf_op args[2]
  11.8 10.7 %project.1 = (f32[256,1536]{1,0:T(8,128)}, f32[256,128]{1,0:T(8,128)}, bf16[2048,1536]{1,0:T(8,128)(2,1)}, bf16[2048,128]{1,0:T(8,128)(2,1)}) custom-call(bf16[256,2048]{1,0:T(8,128)(2,1)} %tok_ref.1, bf16[24576,128]{1,0:T(8,128)(2,1)} %bitcast.249, bf16[8192,15]{1,0:T(8,128)(2,1)} %bitcast.248), custom_call_target="tpu_custom_call" | custom-call | tf_op jit(solution)/shard_map/project/pallas_call | solution.py:83
  22.5 11.0 %local_forward.1 = (bf16[4,256,128]{2,1,0:T(8,128)(2,1)}, bf16[4,256,256]{2,1,0:T(8,128)(2,1)}, bf16[4,256,256]{2,1,0:T(8,128)(2,1)}, bf16[4,256,256]{2,1,0:T(8,...) custom-call(f32[4,2]{1,0:T(4,128)} %copy.10.param_ref, ...), custom_call_target="tpu_custom_call" | custom-call | tf_op jit(solution)/shard_map/local_forward/pallas_call | solution.py:200
  34.5 1.5 collective-permute-start
  36.0 2.9 %collective-permute-start.5 = (bf16[2,4,128,128]{3,2,1,0:T(8,128)(2,1)S(1)}, bf16[2,4,128,128]{3,2,1,0:T(8,128)(2,1)S(1)}, u32[]{:S(2)}, u32[]{:S(2)}) collective-permute-start(bf16[2,4,128,128]{3,2,1,0:T(8,128)(2,1)S(1)} %broadcast_in_dim.86), channel_id=1, source_target_pairs={{0,64},{4,68},{8,72},{12,76},{16,80},{20,84},{24,88},{28,92},{32,9... | collective-permute-start | bytes 786440 | tf_op jit(solution)/shard_map/ppermute | solution.py:385
  40.7 1.4 collective-permute-start.1
  42.3 3.2 %collective-permute-done.5 = bf16[2,4,128,128]{3,2,1,0:T(8,128)(2,1)S(1)} collective-permute-done((bf16[2,4,128,128]{3,2,1,0:T(8,128)(2,1)S(1)}, bf16[2,4,128,128]{3,2,1,0:T(8,128)(2,1)S(1)}, u32[]{:S(2)}, u32[]{:S(2)}) %collective-permute-start.5) | collective-permute-done | bytes 262176 | tf_op jit(solution)/shard_map/ppermute | solution.py:385
  45.7 2.7 %collective-permute-done.1 = bf16[2,4,128,128]{3,2,1,0:T(8,128)(2,1)S(1)} collective-permute-done((bf16[2,4,128,128]{3,2,1,0:T(8,128)(2,1)S(1)}, bf16[2,4,128,128]{3,2,1,0:T(8,128)(2,1)S(1)}, u32[]{:S(2)}, u32[]{:S(2)}) %collective-permute-start.1) | collective-permute-done | bytes 262176 | tf_op jit(solution)/shard_map/ppermute | solution.py:385
  49.2 3.0 %collective-permute-start.2 = (bf16[2,4,128,128]{3,2,1,0:T(8,128)(2,1)S(1)}, bf16[2,4,128,128]{3,2,1,0:T(8,128)(2,1)S(1)}, u32[]{:S(2)}, u32[]{:S(2)}) collective-permute-start(bf16[2,4,128,128]{3,2,1,0:T(8,128)(2,1)S(1)} %pad_maximum_fusion.2), channel_id=1, source_target_pairs={{0,16},{4,20},{8,24},{12,28},{16,0},{20,4},{24,8},{28,12},{32,48},... | collective-permute-start | bytes 786440 | tf_op jit(solution)/shard_map/ppermute | solution.py:385
  52.5 4.9 %collective-permute-done.2 = bf16[2,4,128,128]{3,2,1,0:T(8,128)(2,1)S(1)} collective-permute-done((bf16[2,4,128,128]{3,2,1,0:T(8,128)(2,1)S(1)}, bf16[2,4,128,128]{3,2,1,0:T(8,128)(2,1)S(1)}, u32[]{:S(2)}, u32[]{:S(2)}) %collective-permute-start.2) | collective-permute-done | bytes 262176 | tf_op jit(solution)/shard_map/ppermute | solution.py:385
  59.2 5.2 %collective-permute-done.3 = bf16[2,4,128,128]{3,2,1,0:T(8,128)(2,1)S(1)} collective-permute-done((bf16[2,4,128,128]{3,2,1,0:T(8,128)(2,1)S(1)}, bf16[2,4,128,128]{3,2,1,0:T(8,128)(2,1)S(1)}, u32[]{:S(2)}, u32[]{:S(2)}) %collective-permute-start.3) | collective-permute-done | bytes 262176 | tf_op jit(solution)/shard_map/ppermute | solution.py:385
  66.6 5.3 %collective-permute-done.4 = bf16[2,4,128,128]{3,2,1,0:T(8,128)(2,1)S(1)} collective-permute-done((bf16[2,4,128,128]{3,2,1,0:T(8,128)(2,1)S(1)}, bf16[2,4,128,128]{3,2,1,0:T(8,128)(2,1)S(1)}, u32[]{:S(2)}, u32[]{:S(2)}) %collective-permute-start.4) | collective-permute-done | bytes 262176 | tf_op jit(solution)/shard_map/ppermute | solution.py:385
  73.0 7.3 %out_stage.1 = (bf16[256,2048]{1,0:T(8,128)(2,1)}, bf16[4,256,128]{2,1,0:T(8,128)(2,1)}, bf16[4,256,128]{2,1,0:T(8,128)(2,1)}, bf16[4,640,128]{2,1,0:T(8,128)(2,1)}, f32[256,128]{1,0:T(8,128)}) custom-call(f32[256,128]{1,0:T(8,128)} %get-tuple-element.21.gate_ref, f32[4,256,128]{2,1,0:T(8,128)} %get-tuple-element.23.core_ref, ...), custom_call_target="tpu_custom_call" | custom-call | tf_op jit(solution)/shard_map/out_stage/pallas_call | solution.py:254
  85.3 3.0 %collective-permute-start.10 = (bf16[2,4,128,128]{3,2,1,0:T(8,128)(2,1)S(1)}, bf16[2,4,128,128]{3,2,1,0:T(8,128)(2,1)S(1)}, u32[]{:S(2)}, u32[]{:S(2)}) collective-permute-start(bf16[2,4,128,128]{3,2,1,0:T(8,128)(2,1)S(1)} %fusion.35), channel_id=1, source_target_pairs={{0,16},{4,20},{8,24},{12,28},{16,0},{20,4},{24,8},{28,12},{32,48},... | collective-permute-start | bytes 786440 | tf_op jit(solution)/shard_map/ppermute | solution.py:385
  90.4 5.1 %collective-permute-done.6 = bf16[2,4,128,128]{3,2,1,0:T(8,128)(2,1)S(1)} collective-permute-done((bf16[2,4,128,128]{3,2,1,0:T(8,128)(2,1)S(1)}, bf16[2,4,128,128]{3,2,1,0:T(8,128)(2,1)S(1)}, u32[]{:S(2)}, u32[]{:S(2)}) %collective-permute-start.6) | collective-permute-done | bytes 262176 | tf_op jit(solution)/shard_map/ppermute | solution.py:385
  96.0 1.2 collective-permute-start.8
  97.5 4.2 %collective-permute-done.7 = bf16[2,4,128,128]{3,2,1,0:T(8,128)(2,1)S(1)} collective-permute-done((bf16[2,4,128,128]{3,2,1,0:T(8,128)(2,1)S(1)}, bf16[2,4,128,128]{3,2,1,0:T(8,128)(2,1)S(1)}, u32[]{:S(2)}, u32[]{:S(2)}) %collective-permute-start.7) | collective-permute-done | bytes 262176 | tf_op jit(solution)/shard_map/ppermute | solution.py:385
  102.7 1.8 %collective-permute-done.8 = bf16[2,4,128,128]{3,2,1,0:T(8,128)(2,1)S(1)} collective-permute-done((bf16[2,4,128,128]{3,2,1,0:T(8,128)(2,1)S(1)}, bf16[2,4,128,128]{3,2,1,0:T(8,128)(2,1)S(1)}, u32[]{:S(2)}, u32[]{:S(2)}) %collective-permute-start.8) | collective-permute-done | bytes 262176 | tf_op jit(solution)/shard_map/ppermute | solution.py:385
  105.3 6.0 %collective-permute-done.9 = bf16[2,4,128,128]{3,2,1,0:T(8,128)(2,1)S(1)} collective-permute-done((bf16[2,4,128,128]{3,2,1,0:T(8,128)(2,1)S(1)}, bf16[2,4,128,128]{3,2,1,0:T(8,128)(2,1)S(1)}, u32[]{:S(2)}, u32[]{:S(2)}) %collective-permute-start.9) | collective-permute-done | bytes 262176 | tf_op jit(solution)/shard_map/ppermute | solution.py:385
  114.4 6.1 %collective-permute-done.11 = bf16[2,4,128,128]{3,2,1,0:T(8,128)(2,1)S(1)} collective-permute-done((bf16[2,4,128,128]{3,2,1,0:T(8,128)(2,1)S(1)}, bf16[2,4,128,128]{3,2,1,0:T(8,128)(2,1)S(1)}, u32[]{:S(2)}, u32[]{:S(2)}) %collective-permute-start.11) | collective-permute-done | bytes 262176 | tf_op jit(solution)/shard_map/ppermute | solution.py:385
  121.4 1.5 collective-permute-done.12
  123.0 9.7 %collective-permute-start.13 = (bf16[2,4,128,128]{3,2,1,0:T(8,128)(2,1)S(1)}, bf16[2,4,128,128]{3,2,1,0:T(8,128)(2,1)S(1)}, u32[]{:S(2)}, u32[]{:S(2)}) collective-permute-start(bf16[2,4,128,128]{3,2,1,0:T(8,128)(2,1)S(1)} %fusion.41), channel_id=1, source_target_pairs={{0,4},{4,0},{8,12},{12,8},{16,20},{20,16},{24,28},{28,24},{32,36},... | collective-permute-start | bytes 786440 | tf_op jit(solution)/shard_map/ppermute | solution.py:385
  135.8 15.2 %back_stage.1 = bf16[256,2048]{1,0:T(8,128)(2,1)} custom-call(f32[4,2]{1,0:T(4,128)} %copy.10.param_ref, f32[256,1536]{1,0:T(8,128)} %get-tuple-element.22.proj_ref, f32[256,128]{1,0:T(8,128)} %get-tuple-element.21.gate_ref, f32[256,128]{1,0:T(8,128)} %get-tuple-element.27.clog_ref, bf16[4,256,256]{2,1,0:T(8,128)(2,1)} %get-tuple-element.28.e_ref, ...), custom_call_target="tpu_custom_call" | custom-call | tf_op jit(solution)/shard_map/back_stage/pallas_call | solution.py:374
  151.0 20.9 %reduce-scatter.5.cloned.1.call-done = bf16[256,512]{1,0:T(8,128)(2,1)} async-done(((bf16[256,2048]{1,0:T(8,128)(2,1)}), bf16[256,512]{1,0:T(8,128)(2,1)}) %reduce-scatter.5.cloned.1.call-update) | async-done | bytes 262160 | tf_op jit(solution)/shard_map/reduce_scatter | solution.py:457
  (120 shorter events, 26.5 us)
Async XLA Ops:
  7.2 4.0 %copy-start.5 = (f32[4,2]{0,1:T(2,128)S(1)}, f32[4,2]{0,1:T(2,128)}, u32[]{:S(2)}) copy-start(f32[4,2]{0,1:T(2,128)} %param.10) | copy-start | bytes 100
  7.2 143.8 %reduce-scatter.3.cloned.1.call-start = ((), (), s32[]{:S(2)}) async-start(), calls=%async_computation.2 | async-start | bytes 1310720 | tf_op jit(solution)/shard_map/reduce_scatter | solution.py:432
  33.5 6.6 %copy-start.1 = (bf16[4,256,128]{2,1,0:T(8,128)(2,1)S(1)}, bf16[4,256,128]{2,1,0:T(8,128)(2,1)}, u32[]{:S(2)}) copy-start(bf16[4,256,128]{2,1,0:T(8,128)(2,1)} %get-tuple-element.25) | copy-start | bytes 786436
  34.5 4.5 %collective-permute-start = (bf16[2,4,128,128]{3,2,1,0:T(8,128)(2,1)S(1)}, bf16[2,4,128,128]{3,2,1,0:T(8,128)(2,1)S(1)}, u32[]{:S(2)}, u32[]{:S(2)}) collective-permute-start(bf16[2,4,128,128]{3,2,1,0:T(8,128)(2,1)S(1)} %pad_maximum_fusion), channel_id=1, source_target_pairs={{0,4},{4,0},{8,12},{12,8},{16,20},{20,16},{24,28},{28,24},{32,36},... | collective-permute-start | bytes 786440 | tf_op jit(solution)/shard_map/ppermute | solution.py:385
  36.0 9.4 %collective-permute-start.5 = (bf16[2,4,128,128]{3,2,1,0:T(8,128)(2,1)S(1)}, bf16[2,4,128,128]{3,2,1,0:T(8,128)(2,1)S(1)}, u32[]{:S(2)}, u32[]{:S(2)}) collective-permute-start(bf16[2,4,128,128]{3,2,1,0:T(8,128)(2,1)S(1)} %broadcast_in_dim.86), channel_id=1, source_target_pairs={{0,64},{4,68},{8,72},{12,76},{16,80},{20,84},{24,88},{28,92},{32,9... | collective-permute-start | bytes 786440 | tf_op jit(solution)/shard_map/ppermute | solution.py:385
  39.0 6.5 %copy-start.3 = (bf16[128,128]{1,0:T(8,128)(2,1)}, bf16[128,128]{1,0:T(8,128)(2,1)S(1)}, u32[]{:S(2)}) copy-start(bf16[128,128]{1,0:T(8,128)(2,1)S(1)} %fusion.187) | copy-start | bytes 98308
  40.7 7.6 %collective-permute-start.1 = (bf16[2,4,128,128]{3,2,1,0:T(8,128)(2,1)S(1)}, bf16[2,4,128,128]{3,2,1,0:T(8,128)(2,1)S(1)}, u32[]{:S(2)}, u32[]{:S(2)}) collective-permute-start(bf16[2,4,128,128]{3,2,1,0:T(8,128)(2,1)S(1)} %pad_maximum_fusion.1), channel_id=1, source_target_pairs={{0,8},{4,12},{8,0},{12,4},{16,24},{20,28},{24,16},{28,20},{32,40},... | collective-permute-start | bytes 786440 | tf_op jit(solution)/shard_map/ppermute | solution.py:385
  49.2 8.3 %collective-permute-start.2 = (bf16[2,4,128,128]{3,2,1,0:T(8,128)(2,1)S(1)}, bf16[2,4,128,128]{3,2,1,0:T(8,128)(2,1)S(1)}, u32[]{:S(2)}, u32[]{:S(2)}) collective-permute-start(bf16[2,4,128,128]{3,2,1,0:T(8,128)(2,1)S(1)} %pad_maximum_fusion.2), channel_id=1, source_target_pairs={{0,16},{4,20},{8,24},{12,28},{16,0},{20,4},{24,8},{28,12},{32,48},... | collective-permute-start | bytes 786440 | tf_op jit(solution)/shard_map/ppermute | solution.py:385
  58.3 6.1 %collective-permute-start.3 = (bf16[2,4,128,128]{3,2,1,0:T(8,128)(2,1)S(1)}, bf16[2,4,128,128]{3,2,1,0:T(8,128)(2,1)S(1)}, u32[]{:S(2)}, u32[]{:S(2)}) collective-permute-start(bf16[2,4,128,128]{3,2,1,0:T(8,128)(2,1)S(1)} %pad_maximum_fusion.3), channel_id=1, source_target_pairs={{0,32},{4,36},{8,40},{12,44},{16,48},{20,52},{24,56},{28,60},{32,0... | collective-permute-start | bytes 786440 | tf_op jit(solution)/shard_map/ppermute | solution.py:385
  65.2 6.8 %collective-permute-start.4 = (bf16[2,4,128,128]{3,2,1,0:T(8,128)(2,1)S(1)}, bf16[2,4,128,128]{3,2,1,0:T(8,128)(2,1)S(1)}, u32[]{:S(2)}, u32[]{:S(2)}) collective-permute-start(bf16[2,4,128,128]{3,2,1,0:T(8,128)(2,1)S(1)} %pad_maximum_fusion.4), channel_id=1, source_target_pairs={{0,64},{4,68},{8,72},{12,76},{16,80},{20,84},{24,88},{28,92},{32,9... | collective-permute-start | bytes 786440 | tf_op jit(solution)/shard_map/ppermute | solution.py:385
  72.2 0.9 copy-start.2
  80.3 3.5 %copy-start = (bf16[4,640,128]{2,1,0:T(8,128)(2,1)S(1)}, bf16[4,640,128]{2,1,0:T(8,128)(2,1)}, u32[]{:S(2)}) copy-start(bf16[4,640,128]{2,1,0:T(8,128)(2,1)} %get-tuple-element.36) | copy-start | bytes 1966084
  83.8 88.0 %reduce-scatter.5.cloned.1.call-start = ((), (), s32[]{:S(2)}) async-start(), calls=%async_computation.3 | async-start | bytes 1310720 | tf_op jit(solution)/shard_map/reduce_scatter | solution.py:457
  84.8 5.1 %copy-start.4 = (bf16[128,128]{1,0:T(8,128)(2,1)S(1)}, bf16[128,128]{1,0:T(8,128)(2,1)}, u32[]{:S(2)}) copy-start(bf16[128,128]{1,0:T(8,128)(2,1)} %copy-done.3) | copy-start | bytes 98308
  85.3 27.0 %collective-permute-start.10 = (bf16[2,4,128,128]{3,2,1,0:T(8,128)(2,1)S(1)}, bf16[2,4,128,128]{3,2,1,0:T(8,128)(2,1)S(1)}, u32[]{:S(2)}, u32[]{:S(2)}) collective-permute-start(bf16[2,4,128,128]{3,2,1,0:T(8,128)(2,1)S(1)} %fusion.35), channel_id=1, source_target_pairs={{0,16},{4,20},{8,24},{12,28},{16,0},{20,4},{24,8},{28,12},{32,48},... | collective-permute-start | bytes 786440 | tf_op jit(solution)/shard_map/ppermute | solution.py:385
  88.4 7.1 %collective-permute-start.6 = (bf16[2,4,128,128]{3,2,1,0:T(8,128)(2,1)S(1)}, bf16[2,4,128,128]{3,2,1,0:T(8,128)(2,1)S(1)}, u32[]{:S(2)}, u32[]{:S(2)}) collective-permute-start(bf16[2,4,128,128]{3,2,1,0:T(8,128)(2,1)S(1)} %fusion.33), channel_id=1, source_target_pairs={{0,64},{4,68},{8,72},{12,76},{16,80},{20,84},{24,88},{28,92},{32,9... | collective-permute-start | bytes 786440 | tf_op jit(solution)/shard_map/ppermute | solution.py:385
  95.5 6.1 %collective-permute-start.7 = (bf16[2,4,128,128]{3,2,1,0:T(8,128)(2,1)S(1)}, bf16[2,4,128,128]{3,2,1,0:T(8,128)(2,1)S(1)}, u32[]{:S(2)}, u32[]{:S(2)}) collective-permute-start(bf16[2,4,128,128]{3,2,1,0:T(8,128)(2,1)S(1)} %fusion.38), channel_id=1, source_target_pairs={{0,32},{4,36},{8,40},{12,44},{16,48},{20,52},{24,56},{28,60},{32,0... | collective-permute-start | bytes 786440 | tf_op jit(solution)/shard_map/ppermute | solution.py:385
  96.0 8.4 %collective-permute-start.8 = (bf16[2,4,128,128]{3,2,1,0:T(8,128)(2,1)S(1)}, bf16[2,4,128,128]{3,2,1,0:T(8,128)(2,1)S(1)}, u32[]{:S(2)}, u32[]{:S(2)}) collective-permute-start(bf16[2,4,128,128]{3,2,1,0:T(8,128)(2,1)S(1)} %fusion.34), channel_id=1, source_target_pairs={{0,32},{4,36},{8,40},{12,44},{16,48},{20,52},{24,56},{28,60},{32,0... | collective-permute-start | bytes 786440 | tf_op jit(solution)/shard_map/ppermute | solution.py:385
  104.5 6.8 %collective-permute-start.9 = (bf16[2,4,128,128]{3,2,1,0:T(8,128)(2,1)S(1)}, bf16[2,4,128,128]{3,2,1,0:T(8,128)(2,1)S(1)}, u32[]{:S(2)}, u32[]{:S(2)}) collective-permute-start(bf16[2,4,128,128]{3,2,1,0:T(8,128)(2,1)S(1)} %fusion.39), channel_id=1, source_target_pairs={{0,16},{4,20},{8,24},{12,28},{16,0},{20,4},{24,8},{28,12},{32,48},... | collective-permute-start | bytes 786440 | tf_op jit(solution)/shard_map/ppermute | solution.py:385
  112.4 8.0 %collective-permute-start.11 = (bf16[2,4,128,128]{3,2,1,0:T(8,128)(2,1)S(1)}, bf16[2,4,128,128]{3,2,1,0:T(8,128)(2,1)S(1)}, u32[]{:S(2)}, u32[]{:S(2)}) collective-permute-start(bf16[2,4,128,128]{3,2,1,0:T(8,128)(2,1)S(1)} %fusion.40), channel_id=1, source_target_pairs={{0,8},{4,12},{8,0},{12,4},{16,24},{20,28},{24,16},{28,20},{32,40},... | collective-permute-start | bytes 786440 | tf_op jit(solution)/shard_map/ppermute | solution.py:385
  113.4 9.6 %collective-permute-start.12 = (bf16[2,4,128,128]{3,2,1,0:T(8,128)(2,1)S(1)}, bf16[2,4,128,128]{3,2,1,0:T(8,128)(2,1)S(1)}, u32[]{:S(2)}, u32[]{:S(2)}) collective-permute-start(bf16[2,4,128,128]{3,2,1,0:T(8,128)(2,1)S(1)} %fusion.36), channel_id=1, source_target_pairs={{0,8},{4,12},{8,0},{12,4},{16,24},{20,28},{24,16},{28,20},{32,40},... | collective-permute-start | bytes 786440 | tf_op jit(solution)/shard_map/ppermute | solution.py:385
  123.0 10.8 %collective-permute-start.13 = (bf16[2,4,128,128]{3,2,1,0:T(8,128)(2,1)S(1)}, bf16[2,4,128,128]{3,2,1,0:T(8,128)(2,1)S(1)}, u32[]{:S(2)}, u32[]{:S(2)}) collective-permute-start(bf16[2,4,128,128]{3,2,1,0:T(8,128)(2,1)S(1)} %fusion.41), channel_id=1, source_target_pairs={{0,4},{4,0},{8,12},{12,8},{16,20},{20,16},{24,28},{28,24},{32,36},... | collective-permute-start | bytes 786440 | tf_op jit(solution)/shard_map/ppermute | solution.py:385
  133.1 1.8 %collective-permute-start.14 = (bf16[2,4,128,128]{3,2,1,0:T(8,128)(2,1)S(1)}, bf16[2,4,128,128]{3,2,1,0:T(8,128)(2,1)S(1)}, u32[]{:S(2)}, u32[]{:S(2)}) collective-permute-start(bf16[2,4,128,128]{3,2,1,0:T(8,128)(2,1)S(1)} %fusion.37), channel_id=1, source_target_pairs={{0,4},{4,0},{8,12},{12,8},{16,20},{20,16},{24,28},{28,24},{32,36},... | collective-permute-start | bytes 786440 | tf_op jit(solution)/shard_map/ppermute | solution.py:385
Sparse Core Ops, SparseCore 0:
  83.9 26.3 reduce-scatter.2
  151.1 20.7 reduce-scatter.4

commit v2 on v1

--- a/solution.py
+++ b/solution.py
@@ -245,10 +245,13 @@
         dqh_ref[h] = nn(fg, x).astype(BF)
         gx_ref[h] = tn(fg, qh).astype(BF)
     dlam_ref[...] = dlam
-    part_ref[...] = nn(jnp.concatenate(normed, 1), ow_ref[...]).astype(BF)
-
-
-def out_stage(gate, core, qh, x, gain, grad_out, out_weight, levels, far, near):
+    normed = jnp.concatenate(normed, 1)
+    wide = part_ref.shape[2]
+    for j in range(part_ref.shape[0]):
+        part_ref[j] = nn(normed, ow_ref[:, j * wide : (j + 1) * wide]).astype(BF)
+
+
+def out_stage(gate, core, qh, x, gain, grad_out, out_weight, levels, far, near, groups):
     rows, width = grad_out.shape
     heads = core.shape[0]
     return pl.pallas_call(
@@ -256,7 +259,7 @@
         in_specs=[pl.BlockSpec(memory_space=VM)] * 7,
         out_specs=[pl.BlockSpec(memory_space=VM)] * 5,
         out_shape=[
-            jax.ShapeDtypeStruct((rows, width), BF),
+            jax.ShapeDtypeStruct((groups, rows, width // groups), BF),
             jax.ShapeDtypeStruct((heads, rows, 128), BF),
             jax.ShapeDtypeStruct((heads, rows, 128), BF),
             jax.ShapeDtypeStruct((heads, far * 128, 128), BF),
@@ -267,7 +270,7 @@
 
 
 def back_kernel(heads, levels, group, param_ref, proj_ref, gate_ref, clog_ref, e_ref, s_ref, lp_ref, t_ref, m_ref,
-                nk_ref, g_ref, dqh_ref, dau_ref, dlam_ref, wflat_ref, swflat_ref, part_ref):
+                nk_ref, g_ref, dqh_ref, dau_ref, dlam_ref, dproj_ref, dgate_ref):
     n = proj_ref.shape[0]
     gate = gate_ref[...]
     rate, bias = head_rows(param_ref, heads, n)
@@ -360,49 +363,347 @@
     dstep = lax.dot_general(upper, dlog, (((1,), (0,)), ((), ())),
                             precision=lax.Precision.HIGHEST, preferred_element_type=F32)
     dgate = dlam * sig_all - rate * sig_all * (1.0 - sig_all) * dstep + beta_all * (1.0 - beta_all) * dbeta_all
-    dgate = dgate.astype(BF)
-    dproj = jnp.concatenate(out, 1)
-    width = part_ref.shape[1]
-    for j in range(0, width, 512):
-        part = nt(dproj, wflat_ref[j : j + 512, :]) + nt(dgate, swflat_ref[j : j + 512, :])
-        part_ref[:, j : j + 512] = part.astype(BF)
-
-
-def back_stage(head_param, proj, gate, clog, saved, g, dqh, dau, dlam, wflat, swflat, levels):
+    dgate_ref[...] = dgate.astype(BF)
+    for j, grad in enumerate(out):
+        dproj_ref[:, j * 128 : (j + 1) * 128] = grad
+
+
+def back_stage(head_param, proj, gate, clog, saved, g, dqh, dau, dlam, levels):
     rows = proj.shape[0]
     heads = head_param.shape[0]
     return pl.pallas_call(
         functools.partial(back_kernel, heads, levels, 1),
-        in_specs=[pl.BlockSpec(memory_space=pltpu.SMEM)] + [pl.BlockSpec(memory_space=VM)] * 15,
+        in_specs=[pl.BlockSpec(memory_space=pltpu.SMEM)] + [pl.BlockSpec(memory_space=VM)] * 13,
+        out_specs=[pl.BlockSpec(memory_space=VM)] * 2,
+        out_shape=[jax.ShapeDtypeStruct((rows, 3 * heads * 128), BF), jax.ShapeDtypeStruct((rows, heads * LANES), BF)],
+        name="back_stage",
+    )(head_param, proj, gate, clog, *saved, g, dqh, dau, dlam)
+
+
+MESH = pl.DeviceIdType.MESH
+RING = 4
+
+
+def place():
+    ctx = lax.axis_index("ctx")
+    return lax.div(ctx, 2 * RING), lax.rem(lax.div(ctx, 2), RING), lax.rem(ctx, 2)
+
+
+def at_ctx(x, y, core):
+    return {"ctx": (x * RING + y) * 2 + core}
+
+
+def around(index, step):
+    return lax.rem(index + step + RING, RING)
+
+
+def greet(peers):
+    barrier = pltpu.get_barrier_semaphore()
+    for peer in peers:
+        pl.semaphore_signal(barrier, inc=1, device_id=peer, device_id_type=MESH)
+    pl.semaphore_wait(barrier, len(peers))
+
+
+def remote(src, dst, send, recv, index, peer):
+    return pltpu.make_async_remote_copy(
+        src_ref=src, dst_ref=dst, send_sem=send.at[index], recv_sem=recv.at[index],
+        device_id=peer, device_id_type=MESH)
+
+
+def ring_start(buf, send, recv, base, right, left, low=0):
+    rows = pl.ds(low, buf.shape[2] - low)
+    copies = [
+        remote(buf.at[0, 0, rows], buf.at[1, 0, rows], send, recv, base, right),
+        remote(buf.at[0, 1], buf.at[3, 1], send, recv, base + 1, left),
+        remote(buf.at[0, 1, rows], buf.at[1, 1, rows], send, recv, base + 2, right),
+        remote(buf.at[0, 0], buf.at[3, 0], send, recv, base + 3, left),
+    ]
+    for copy in copies:
+        copy.start()
+    return copies
+
+
+def ring_finish(copies, buf, send, recv, base, right, left, low=0):
+    rows = pl.ds(low, buf.shape[2] - low)
+    copies[0].wait_recv()
+    on_right = remote(buf.at[1, 0, rows], buf.at[2, 0, rows], send, recv, base + 4, right)
+    on_right.start()
+    copies[1].wait_recv()
+    on_left = remote(buf.at[3, 1, rows], buf.at[2, 1, rows], send, recv, base + 5, left)
+    on_left.start()
+    copies[2].wait_recv()
+    copies[3].wait_recv()
+    on_right.wait_recv()
+    on_left.wait_recv()
+    for copy in copies + [on_right, on_left]:
+        copy.wait_send()
+
+
+def flag(cond):
+    return jnp.where(cond, 1.0, 0.0).astype(F32)
+
+
+def gather_kernel(au_ref, x_ref, cores_ref, ys_ref, xs_ref, cores, ys, xs, share, send, recv, local):
+    x, y, core = place()
+    partner = at_ctx(x, y, 1 - core)
+    y_right, y_left = at_ctx(x, around(y, 1), core), at_ctx(x, around(y, -1), core)
+    x_right, x_left = at_ctx(around(x, 1), y, core), at_ctx(around(x, -1), y, core)
+    greet((partner, y_right, y_left, x_right, x_left))
+    swap = remote(au_ref, cores.at[1], send, recv, 0, partner)
+    swap.start()
+    keep = pltpu.make_async_copy(au_ref, cores.at[0], local.at[0])
+    keep.start()
+    keep.wait()
+    swap.wait_recv()
+    first = core * 2
+    low_slot, high_slot = core, 1 - core
+    eye_r, eye_c = iotas(128, 128)
+    eye = jnp.where(eye_r == eye_c, 1.0, 0.0).astype(F32)
+    top = lax.broadcasted_iota(jnp.int32, (256, 128), 0) < 128
+
+    def joined(below, above):
+        return nn(below, above[128:256]) + jnp.where(top, above.astype(F32), 0.0)
+
+    for i in range(2):
+        ys[0, i] = joined(cores[low_slot, first + i], cores[high_slot, first + i]).astype(BF)
+    copies = ring_start(ys, send, recv, 1, y_right, y_left)
+    ring_finish(copies, ys, send, recv, 1, y_right, y_left)
+    prefix = [None, None]
+    for i in range(2):
+        at = [ys[around(y, -k), i] for k in range(RING)]
+        s1 = joined(at[0], at[1])
+        s2 = joined(s1.astype(BF), at[2])
+        s3 = joined(s2.astype(BF), at[3])
+        xs[0, i] = s3.astype(BF)
+        x1 = flag(lax.rem(y, 2) == 1) * ys[1, i, 0:128].astype(F32)
+        s1u = s1[0:128]
+        x2 = flag(y == 2) * s1u + flag(y == 3) * nn(s1u.astype(BF), at[2][128:256])
+        share[first + i, 0:128] = x1.astype(BF)
+        share[first + i, 128:256] = x2.astype(BF)
+        prefix[i] = (flag(y == 0) * eye + flag(y == 1) * at[0][128:256].astype(F32)
+                     + flag(y == 2) * s1[128:256] + flag(y == 3) * s2[128:256]).astype(BF)
+    copies = ring_start(xs, send, recv, 7, x_right, x_left)
+    ring_finish(copies, xs, send, recv, 7, x_right, x_left)
+    for i in range(2):
+        at = [xs[around(x, -k), i] for k in range(RING)]
+        r1 = nn(at[0][0:128], at[1][128:256]) + at[1][0:128].astype(F32)
+        x3 = flag(lax.rem(x, 2) == 1) * xs[1, i, 0:128].astype(F32)
+        x4 = flag(x == 2) * r1 + flag(x == 3) * nn(r1.astype(BF), at[2][128:256])
+        both = jnp.concatenate([x3.astype(BF), x4.astype(BF)], 0)
+        share[first + i, 256:512] = nn(both, prefix[i]).astype(BF)
+    give = remote(share.at[pl.ds(first, 2)], share.at[pl.ds(first, 2)], send, recv, 13, partner)
+    take = remote(share.at[pl.ds(2 - first, 2)], share.at[pl.ds(2 - first, 2)], send, recv, 13, partner)
+    give.start()
+    upper = flag(core == 1)
+    swap.wait_send()
+    step = []
+    for h in range(4):
+        below = cores[low_slot, h]
+        x_ref[h, 0:128] = (upper * below[0:128].astype(F32)).astype(BF)
+        step.append((upper * below[128:256].astype(F32) + (1.0 - upper) * eye).astype(BF))
+    cores_ref[...] = cores[...]
+    ys_ref[...] = ys[...]
+    xs_ref[...] = xs[...]
+    take.wait_recv()
+    give.wait_send()
+    for h in range(4):
+        x_ref[h, 128:640] = nn(share[h], step[h]).astype(BF)
+
+
+def gather_states(au):
+    heads = au.shape[0]
+    cores = ((2, heads, 256, 128), BF)
+    ring = ((RING, 2, 256, 128), BF)
+    return pl.pallas_call(
+        gather_kernel,
+        in_specs=[pl.BlockSpec(memory_space=VM)],
+        out_specs=[pl.BlockSpec(memory_space=VM)] * 4,
+        out_shape=[jax.ShapeDtypeStruct((heads, 640, 128), BF)] + [jax.ShapeDtypeStruct(*s) for s in (cores, ring, ring)],
+        scratch_shapes=[VM(*cores), VM(*ring), VM(*ring), VM((heads, 512, 128), BF),
+                        pltpu.SemaphoreType.DMA((14,)), pltpu.SemaphoreType.DMA((14,)), pltpu.SemaphoreType.DMA((1,))],
+        compiler_params=pltpu.CompilerParams(collective_id=1, has_side_effects=True),
+        name="gather_states",
+    )(au)
+
+
+def return_kernel(groups, gx_ref, x_ref, cores_ref, ys_ref, xs_ref, part_ref, dau_ref, layer_ref,
+                  mine, other, ys, xs, share, chunks, send, recv, zsend, zrecv):
+    x, y, core = place()
+    z = lax.axis_index("head")
+    partner = at_ctx(x, y, 1 - core)
+    y_right, y_left = at_ctx(x, around(y, 1), core), at_ctx(x, around(y, -1), core)
+    x_right, x_left = at_ctx(around(x, 1), y, core), at_ctx(around(x, -1), y, core)
+    across = [{"head": lax.rem(z + k, groups)} for k in range(1, groups)]
+    greet([partner, y_right, y_left, x_right, x_left] + across)
+    first = core * 2
+    rest = 2 - first
+    swap = remote(gx_ref.at[pl.ds(rest, 2)], mine, send, recv, 0, partner)
+    swap.start()
+    swap_rest = remote(gx_ref.at[pl.ds(first, 2)], other, send, recv, 1, partner)
+    swap_rest.start()
+    spread = []
+    for k in range(1, groups):
+        to = lax.rem(z + k, groups)
+        spread.append(remote(part_ref.at[to], chunks.at[k - 1], zsend, zrecv, k - 1, across[k - 1]))
+        spread[-1].start()
+    low_slot, high_slot = core, 1 - core
+    upper = flag(core == 1)
+    bits = [flag(core == 1), flag(lax.rem(y, 2) == 1), flag(y >= 2), flag(lax.rem(x, 2) == 1), flag(x >= 2)]
+    eye_r, eye_c = iotas(128, 128)
+    eye = jnp.where(eye_r == eye_c, 1.0, 0.0).astype(F32)
+    level = lax.div(lax.broadcasted_iota(jnp.int32, (512, 128), 0), 128)
+    mask = jnp.where(level == 0, bits[1], jnp.where(level == 1, bits[2], jnp.where(level == 2, bits[3], bits[4])))
+    swap.wait_recv()
+    for i in range(2):
+        here = gx_ref[first + i, 128:640]
+        there = mine[i, 128:640]
+        high = (upper * here.astype(F32) + (1.0 - upper) * there.astype(F32)).astype(BF)
+        low = (1.0 - upper) * here.astype(F32) + upper * there.astype(F32)
+        ys[0, i] = (mask * (low + nt(high, cores_ref[low_slot, first + i, 128:256]))).astype(BF)
+    copies = ring_start(ys, send, recv, 2, y_right, y_left, 128)
+    after = [None, None]
+    for i in range(2):
+        at = [ys_ref[around(y, -k), i, 128:256] for k in range(RING)]
+        q1 = nn(at[2], at[3])
+        q0 = nn(at[1], q1.astype(BF))
+        after[i] = (flag(y == 3) * eye + flag(y == 2) * at[3].astype(F32) + flag(y == 1) * q1 + flag(y == 0) * q0).astype(BF)
+    ring_finish(copies, ys, send, recv, 2, y_right, y_left, 128)
+    held = [None, None]
+    for i in range(2):
+        trans = [ys_ref[around(y, -k), i, 128:256] for k in range(RING)]
+        at = [ys[around(y, -k), i, 128:512] for k in range(RING)]
+        h1 = nt(at[3], trans[2]) + at[2].astype(F32)
+        h0 = nt(h1.astype(BF), trans[1]) + at[1].astype(F32)
+        column = nt(h0[128:384].astype(BF), trans[0]) + at[0][128:384].astype(F32)
+        xs[0, i] = column.astype(BF)
+        held[i] = flag(y == 2) * at[3].astype(F32) + flag(y == 1) * h1 + flag(y == 0) * h0
+        share[first + i, 0:128] = ((1.0 - bits[1]) * ys[3, i, 0:128].astype(F32)).astype(BF)
+        share[first + i, 128:256] = held[i][0:128].astype(BF)
+    copies = ring_start(xs, send, recv, 8, x_right, x_left)
+    ring_finish(copies, xs, send, recv, 8, x_right, x_left)
+    for i in range(2):
+        trans = [xs_ref[around(x, -k), i, 128:256] for k in range(RING)]
+        at = [xs[around(x, -k), i, 128:256] for k in range(RING)]
+        h1 = nt(at[3], trans[2]) + at[2].astype(F32)
+        h0 = nt(h1.astype(BF), trans[1]) + at[1].astype(F32)
+        v4 = flag(x == 2) * at[3].astype(F32) + flag(x == 1) * h1 + flag(x == 0) * h0
+        v3 = (1.0 - bits[3]) * xs[3, i, 0:128].astype(F32)
+        both = jnp.concatenate([v3.astype(BF), v4.astype(BF)], 0)
+        share[first + i, 256:512] = (held[i][128:384] + nt(both, after[i])).astype(BF)
+    give = remote(share.at[pl.ds(first, 2)], share.at[pl.ds(first, 2)], send, recv, 14, partner)
+    take = remote(share.at[pl.ds(rest, 2)], share.at[pl.ds(rest, 2)], send, recv, 14, partner)
+    give.start()
+    swap_rest.wait_recv()
+    take.wait_recv()
+    give.wait_send()
+    for h in range(4):
+        mine_here = flag(core == h // 2)
+        got = mine_here * mine[h % 2].astype(F32) + (1.0 - mine_here) * other[h % 2].astype(F32)
+        got = (1.0 - upper) * got
+        v0 = got[0:128]
+        move = (upper * eye + (1.0 - upper) * cores_ref[high_slot, h, 128:256].astype(F32)).astype(BF)
+        v = nt(share[h], move) + mask * got[128:640]
+        parts = [v0] + [v[k * 128 : (k + 1) * 128] for k in range(4)]
+        so_far = jnp.zeros((128, 128), F32)
+        du = jnp.zeros((128, 128), F32)
+        states = []
+        for k in range(5):
+            state = x_ref[h, k * 128 : (k + 1) * 128].astype(F32)
+            states.append((bits[k] * state + (1.0 - bits[k]) * so_far).astype(BF))
+            so_far = so_far + state
+            du = du + (1.0 - bits[k]) * parts[k]
+        da = tn(jnp.concatenate(states, 0), jnp.concatenate([v0, v], 0).astype(BF))
+        dau_ref[h, 0:128] = du.astype(BF)
+        dau_ref[h, 128:256] = da.astype(BF)
+    total = part_ref[z].astype(F32)
+    for copy in spread:
+        copy.wait_recv()
+    for k in range(groups - 1):
+        total = total + chunks[k].astype(F32)
+    layer_ref[...] = total.astype(BF)
+    for copy in [swap, swap_rest] + spread:
+        copy.wait_send()
+
+
+def return_grads(gx, x, cores, ys, xs, part):
+    heads = gx.shape[0]
+    groups, rows, wide = part.shape
+    ring = (RING, 2)
+    return pl.pallas_call(
+        functools.partial(return_kernel, groups),
+        in_specs=[pl.BlockSpec(memory_space=VM)] * 6,
+        out_specs=[pl.BlockSpec(memory_space=VM)] * 2,
+        out_shape=[jax.ShapeDtypeStruct((heads, 256, 128), BF), jax.ShapeDtypeStruct((rows, wide), BF)],
+        scratch_shapes=[VM((2, 640, 128), BF), VM((2, 640, 128), BF), VM(ring + (512, 128), BF), VM(ring + (256, 128), BF),
+                        VM((heads, 512, 128), BF), VM((3, rows, wide), BF),
+                        pltpu.SemaphoreType.DMA((15,)), pltpu.SemaphoreType.DMA((15,)),
+                        pltpu.SemaphoreType.DMA((3,)), pltpu.SemaphoreType.DMA((3,))],
+        compiler_params=pltpu.CompilerParams(collective_id=2, has_side_effects=True),
+        name="return_grads",
+    )(gx, x, cores, ys, xs, part)
+
+
+def last_kernel(groups, dproj_ref, dgate_ref, w_ref, sw_ref, out_ref, mine, relay, direct, extra, arrive, send, recv):
+    rows, wide = out_ref.shape
+    z = lax.axis_index("head")
+    half = wide // 2
+    right, left = {"head": lax.rem(z + 1, groups)}, {"head": lax.rem(z + groups - 1, groups)}
+    greet((right, left))
+    dproj, dgate = dproj_ref[...], dgate_ref[...]
+
+    def product(step):
+        chunk = lax.rem(z + step + groups, groups)
+        at = pl.ds(pl.multiple_of(chunk * wide, wide), wide)
+        return nt(dproj, w_ref[at, :]) + nt(dgate, sw_ref[at, :])
+
+    far = product(2)
+    relay[0] = far[:, :half].astype(BF)
+    relay[1] = far[:, half:].astype(BF)
+    far_right = remote(relay.at[0], arrive.at[0], send, recv, 0, right)
+    far_left = remote(relay.at[1], arrive.at[1], send, recv, 1, left)
+    far_right.start()
+    far_left.start()
+    to_right = product(1)
+    direct[0] = to_right[:, half:].astype(BF)
+    near_right = remote(direct.at[0], arrive.at[2], send, recv, 2, right)
+    near_right.start()
+    to_left = product(-1)
+    direct[1] = to_left[:, :half].astype(BF)
+    near_left = remote(direct.at[1], arrive.at[3], send, recv, 3, left)
+    near_left.start()
+    far_right.wait_recv()
+    extra[0] = (to_right[:, :half] + arrive[0].astype(F32)).astype(BF)
+    sum_right = remote(extra.at[0], arrive.at[4], send, recv, 4, right)
+    sum_right.start()
+    far_left.wait_recv()
+    extra[1] = (to_left[:, half:] + arrive[1].astype(F32)).astype(BF)
+    sum_left = remote(extra.at[1], arrive.at[5], send, recv, 5, left)
+    sum_left.start()
+    mine[...] = product(0)
+    near_right.wait_recv()
+    near_left.wait_recv()
+    sum_right.wait_recv()
+    sum_left.wait_recv()
+    out_ref[:, :half] = (mine[:, :half] + arrive[4].astype(F32) + arrive[3].astype(F32)).astype(BF)
+    out_ref[:, half:] = (mine[:, half:] + arrive[5].astype(F32) + arrive[2].astype(F32)).astype(BF)
+    for copy in (far_right, far_left, near_right, near_left, sum_right, sum_left):
+        copy.wait_send()
+
+
+def last_stage(dproj, dgate, wflat, swflat, groups):
+    rows = dproj.shape[0]
+    wide = wflat.shape[0] // groups
+    half = (rows, wide // 2)
+    return pl.pallas_call(
+        functools.partial(last_kernel, groups),
+        in_specs=[pl.BlockSpec(memory_space=VM)] * 4,
         out_specs=pl.BlockSpec(memory_space=VM),
-        out_shape=jax.ShapeDtypeStruct((rows, wflat.shape[0]), BF),
-        compiler_params=pltpu.CompilerParams(vmem_limit_bytes=60 * 2**20),
-        name="back_stage",
-    )(head_param, proj, gate, clog, *saved, g, dqh, dau, dlam, wflat, swflat)
-
-
-def swapped(array, axis, stride):
-    return lax.ppermute(array, axis, [(i, i ^ 1 << stride) for i in range(lax.axis_size(axis))])
-
-
-def mat_mul(left, right):
-    return jnp.matmul(left, right)
-
-
-def flip_last(array_in):
-    return jnp.swapaxes(array_in, -1, -2)
-
-
-def merge_step(pair_now, prefix, pair_peer, is_upper):
-    a_now = pair_now[0]
-    u_now = pair_now[1]
-    a_peer = pair_peer[0]
-    u_peer = pair_peer[1]
-    arriving = jnp.where(is_upper, mat_mul(u_peer, prefix), 0.0)
-    new_prefix = jnp.where(is_upper, mat_mul(a_peer, prefix), prefix)
-    new_a = jnp.where(is_upper, mat_mul(a_peer, a_now), mat_mul(a_now, a_peer))
-    new_u = jnp.where(is_upper, mat_mul(u_peer, a_now) + u_now, mat_mul(u_now, a_peer) + u_peer)
-    return (arriving, new_prefix, jnp.stack([new_a, new_u], 0))
+        out_shape=jax.ShapeDtypeStruct((rows, wide), BF),
+        scratch_shapes=[VM((rows, wide), F32), VM((2,) + half, BF), VM((2,) + half, BF), VM((2,) + half, BF),
+                        VM((6,) + half, BF), pltpu.SemaphoreType.DMA((6,)), pltpu.SemaphoreType.DMA((6,))],
+        compiler_params=pltpu.CompilerParams(collective_id=3, has_side_effects=True),
+        name="last_stage",
+    )(dproj, dgate, wflat, swflat)
 
 
 def on_device(tokens, qkv_weight, small_weight, head_param, norm_gain, out_weight, grad_out):
@@ -411,50 +712,16 @@
     levels = small_weight.shape[2] - 2
     near = (rows // 64).bit_length()
     far = lax.axis_size("ctx").bit_length() - 1
-    index_ctx = lax.axis_index("ctx")
+    groups = lax.axis_size("head")
     proj, gate, wflat, swflat = project(tokens, qkv_weight, small_weight)
     au, *saved, core, qh, clog = local_forward(head_param, proj, gate, levels)
-    au = au.astype(F32)
-    pair_now = jnp.stack([au[:, 128:], au[:, :128]], 0)
-    prefix = jnp.broadcast_to(jnp.eye(128, dtype=jnp.float32), (heads, 128, 128))
-    saved_steps = []
-    incoming = []
-    for bit_no in range(far):
-        pair_peer = swapped(pair_now.astype(BF), "ctx", bit_no).astype(F32)
-        is_upper = index_ctx // 2**bit_no % 2 == 1
-        saved_steps.append((pair_now, prefix, is_upper))
-        arriving, prefix, pair_now = merge_step(pair_now, prefix, pair_peer, is_upper)
-        incoming.append(arriving)
-    x = jnp.concatenate(incoming, 1).astype(BF)
-    out_part, g, dqh, gx, dlam = out_stage(
+    x, cores, ys, xs = gather_states(au)
+    part, g, dqh, gx, dlam = out_stage(
         gate, core, qh, x, norm_gain.reshape(1, -1), grad_out, out_weight.reshape(heads * 128, width),
-        levels, far, near)
-    layer_out = lax.psum_scatter(out_part, "head", scatter_dimension=1, tiled=True)
-    gx = gx.astype(F32)
-    grad_incoming = [gx[:, i * 128 : (i + 1) * 128] for i in range(far)]
-    grad_pair = jnp.zeros_like(pair_now)
-    grad_prefix = jnp.zeros(prefix.shape, F32)
-    for bit_no in reversed(range(far)):
-        pair_now, prefix, is_upper = saved_steps[bit_no]
-        grad_arrived = grad_incoming[bit_no]
-        through = jnp.stack(
-            [mat_mul(grad_prefix, flip_last(prefix)), mat_mul(grad_arrived, flip_last(prefix))], 0)
-        through = jnp.where(is_upper, through, 0.0)
-        pair_peer, peer_grad, peer_through = (
-            swapped(pair_now.astype(BF), "ctx", bit_no).astype(F32),
-            swapped(grad_pair.astype(BF), "ctx", bit_no).astype(F32),
-            swapped(through.astype(BF), "ctx", bit_no).astype(F32),
-        )
-
-        def step_local(pair_in, prefix_in, peer_in):
-            return merge_step(pair_in, prefix_in, peer_in, is_upper)
-
-        step_out, pull_step = jax.vjp(step_local, pair_now, prefix, pair_peer)
-        own_part, grad_prefix, unused_peer = pull_step((grad_arrived, grad_prefix, grad_pair + peer_grad))
-        grad_pair = own_part + peer_through
-    dau = jnp.concatenate([grad_pair[1], grad_pair[0]], 1).astype(BF)
-    grad_part = back_stage(head_param, proj, gate, clog, saved, g, dqh, dau, dlam, wflat, swflat, levels)
-    grad_tokens = lax.psum_scatter(grad_part, "head", scatter_dimension=1, tiled=True)
+        levels, far, near, groups)
+    dau, layer_out = return_grads(gx, x, cores, ys, xs, part)
+    dproj, dgate = back_stage(head_param, proj, gate, clog, saved, g, dqh, dau, dlam, levels)
+    grad_tokens = last_stage(dproj, dgate, wflat, swflat, groups)
     return (layer_out, grad_tokens)
 
 

time: 180 us -> 123 us (0.68)
  Pallas kernels: 44.1 us -> 114 us
  waiting for transfers between devices: 67.3 us -> 0 us
  starting transfers between devices: 27.5 us -> 0 us
  matrix products: 16.5 us -> 0 us
  between operations: 14.8 us -> 0.67 us
  other arithmetic: 1.91 us -> 0 us
    pallas_call x0 -> x3, Pallas kernels: none -> 73.7 us  [the longest x1 30.9 us: return_grads(): pl.pallas_call(functools.partial(return_kernel, groups), in_specs=[pl.Blo...]
    ppermute x15 -> x0, waiting for transfers between devices: 46.4 us -> none  [swapped(): lax.ppermute(array, axis, [(i, i ^ 1 << stride) for i in range(lax.axis_s...]
    ppermute x15 -> x0, starting transfers between devices: 27.4 us -> none  [swapped(): lax.ppermute(array, axis, [(i, i ^ 1 << stride) for i in range(lax.axis_s...]
    reduce_scatter x2 -> x0, waiting for transfers between devices: 20.9 us -> none  [the longest x1 20.9 us: on_device(): lax.psum_scatter(grad_part, 'head', scatter_dimension=1, tiled=True)]
    dot_general x62 -> x0, matrix products: 16.5 us -> none  [mat_mul(): return jnp.matmul(left, right)]
    pallas_call x1, Pallas kernels: 15.2 us -> 11.4 us  [back_stage(): pl.pallas_call(functools.partial(back_kernel, heads, levels, 1), in_specs...]
    unnamed x14 -> x6, local copies, waits for them, and re-layouts: 5.46 us -> 7.65 us
  transfers between devices with their start and end apart: 17 -> 0, of which waited for: 14 -> 0; matrix products, arithmetic and copies ran while one was open for 7% -> 0% of each run, Pallas kernels for 8% -> 0%
where the time goes in v2:
time: 123 us; the launch traced here: 122 us
  Pallas kernels  114 us (93%)
  local copies, waits for them, and re-layouts  7.65 us (6%)
    pallas_call x1, Pallas kernels, return_grads(): pl.pallas_call(functools.partial(return_kernel, groups), in_specs=[pl.Blo...  30.9 us
    pallas_call x1, Pallas kernels, gather_states(): pl.pallas_call(gather_kernel, in_specs=[pl.BlockSpec(memory_space=VM)], o...  26.3 us
    pallas_call x1, Pallas kernels, last_stage(): pl.pallas_call(functools.partial(last_kernel, groups), in_specs=[pl.Block...  16.5 us
    pallas_call x1, Pallas kernels, back_stage(): pl.pallas_call(functools.partial(back_kernel, heads, levels, 1), in_specs...  11.4 us
    pallas_call x1, Pallas kernels, local_forward(): pl.pallas_call(functools.partial(local_kernel, heads, levels, group), in_...  11 us
    pallas_call x1, Pallas kernels, project(): pl.pallas_call(functools.partial(proj_kernel, heads, extra), grid=(width...  10.7 us
    unnamed x6, local copies, waits for them, and re-layouts  7.65 us
    pallas_call x1, Pallas kernels, out_stage(): pl.pallas_call(functools.partial(out_kernel, heads, levels, far, near), i...  7.31 us

profile of v2, /device:TPU:1, one launch (start us, length us, event | category | flops | bytes accessed | tf_op | source)
XLA Modules:
  0.0 122.5 jit_solution(16329116290280867903)
XLA Ops:
  0.6 1.3 %copy.10.param_ref = f32[4,2]{1,0:T(4,128)} copy(f32[4,2]{0,1:T(2,128)} %param.10) | data formatting | bytes 64 | tf_op args[3]
  2.0 3.9 %copy.9 = bf16[2048,4,15]{2,1,0:T(4,128)(2,1)} copy(bf16[2048,4,15]{0,1,2:T(4,128)(2,1)} %param.9) | data formatting | bytes 491520 | tf_op args[2]
  5.9 10.7 %project.1 = (f32[256,1536]{1,0:T(8,128)}, f32[256,128]{1,0:T(8,128)}, bf16[2048,1536]{1,0:T(8,128)(2,1)}, bf16[2048,128]{1,0:T(8,128)(2,1)}) custom-call(bf16[256,2048]{1,0:T(8,128)(2,1)} %tok_ref.1, bf16[24576,128]{1,0:T(8,128)(2,1)} %bitcast.5, bf16[8192,15]{1,0:T(8,128)(2,1)} %bitcast.4), custom_call_target="tpu_custom_call" | custom-call | tf_op jit(solution)/shard_map/project/pallas_call | solution.py:83
  16.6 11.0 %local_forward.1 = (bf16[4,256,128]{2,1,0:T(8,128)(2,1)}, bf16[4,256,256]{2,1,0:T(8,128)(2,1)}, bf16[4,256,256]{2,1,0:T(8,128)(2,1)}, bf16[4,256,256]{2,1,0:T(8,...) custom-call(f32[4,2]{1,0:T(4,128)} %copy.10.param_ref, ...), custom_call_target="tpu_custom_call" | custom-call | tf_op jit(solution)/shard_map/local_forward/pallas_call | solution.py:200
  27.6 26.3 %gather_states.1 = (bf16[4,640,128]{2,1,0:T(8,128)(2,1)}, bf16[2,4,256,128]{3,2,1,0:T(8,128)(2,1)}, bf16[4,2,256,128]{3,2,1,0:T(8,128)(2,1)}, bf16[4,2,256,128]{3,2,1,0:T(8,128)(2,1)}) custom-call(bf16[4,256,128]{2,1,0:T(8,128)(2,1)} %get-tuple-element.33.au_ref), custom_call_target="tpu_custom_call" | custom-call | tf_op jit(solution)/shard_map/gather_states/pallas_call | solution.py:517
  53.9 7.3 %out_stage.1 = (bf16[4,256,512]{2,1,0:T(8,128)(2,1)}, bf16[4,256,128]{2,1,0:T(8,128)(2,1)}, bf16[4,256,128]{2,1,0:T(8,128)(2,1)}, bf16[4,640,128]{2,1,0:T(8,128)(2,1)}, f32[256,128]{1,0:T(8,128)}) custom-call(f32[256,128]{1,0:T(8,128)} %get-tuple-element.29.gate_ref, f32[4,256,128]{2,1,0:T(8,128)} %get-tuple-element.31.core_ref, ...), custom_call_target="tpu_custom_call" | custom-call | tf_op jit(solution)/shard_map/out_stage/pallas_call | solution.py:257
  61.3 30.9 %return_grads.1 = (bf16[4,256,128]{2,1,0:T(8,128)(2,1)}, bf16[256,512]{1,0:T(8,128)(2,1)}) custom-call(bf16[4,640,128]{2,1,0:T(8,128)(2,1)} %get-tuple-element.35.gx_ref, bf16[4,640,128]{2,1,0:T(8,128)(2,1)} %get-tuple-element.34.x_ref, bf16[2,4,256,128]{3,2,1,0:T(8,128)(2,1)} %get-tuple-element.36.cores_ref, ...), custom_call_target="tpu_custom_call" | custom-call | tf_op jit(solution)/shard_map/return_grads/pallas_call | solution.py:632
  92.2 11.4 %back_stage.1 = (bf16[256,1536]{1,0:T(8,128)(2,1)}, bf16[256,128]{1,0:T(8,128)(2,1)}) custom-call(f32[4,2]{1,0:T(4,128)} %copy.10.param_ref, f32[256,1536]{1,0:T(8,128)} %get-tuple-element.30.proj_ref, f32[256,128]{1,0:T(8,128)} %get-tuple-element.29.gate_ref, f32[256,128]{1,0:T(8,128)} %get-tuple-element.41.clog_ref, ...), custom_call_target="tpu_custom_call" | custom-call | tf_op jit(solution)/shard_map/back_stage/pallas_call | solution.py:374
  103.6 0.0 copy-start
  103.6 16.5 %last_stage.1 = bf16[256,512]{1,0:T(8,128)(2,1)} custom-call(bf16[256,1536]{1,0:T(8,128)(2,1)} %get-tuple-element.52.dproj_ref, bf16[256,128]{1,0:T(8,128)(2,1)} %get-tuple-element.53.dgate_ref, bf16[2048,1536]{1,0:T(8,128)(2,1)} %get-tuple-element.54.w_ref, bf16[2048,128]{1,0:T(8,128)(2,1)} %get-tuple-element.55.sw_ref), custom_call_target="tpu_custom_call" | custom-call | tf_op jit(solution)/shard_map/last_stage/pallas_call | solution.py:697
  120.1 0.0 copy-done
  120.1 0.7 copy.14
  120.8 1.7 %copy.15 = bf16[256,512]{1,0:T(8,128)(2,1)} copy(bf16[256,512]{1,0:T(8,128)(2,1)} %last_stage.1) | data formatting | bytes 524288
Async XLA Ops:
  103.6 16.5 %copy-start = (bf16[256,512]{1,0:T(8,128)(2,1)S(1)}, bf16[256,512]{1,0:T(8,128)(2,1)}, u32[]{:S(2)}) copy-start(bf16[256,512]{1,0:T(8,128)(2,1)} %get-tuple-element.58) | copy-start | bytes 786436

commit v3 on v2

v3 whole, which is shorter than its diff:
```python
import functools

import jax
import jax.numpy as jnp
from jax import lax
from jax.experimental import pallas as pl
from jax.experimental.pallas import tpu as pltpu
from jax.sharding import PartitionSpec as P

BF = jnp.bfloat16
F32 = jnp.float32
LANES = 32
LIMIT = {"project": 44, "local": 24, "gather": 16, "out": 16, "return": 20, "back": 24, "last": 24}


def lane_of(h, level, heads):
    return level * heads + h
VM = pltpu.VMEM


def nn(a, b):
    return lax.dot_general(a, b, (((1,), (0,)), ((), ())), preferred_element_type=F32)


def nt(a, b):
    return lax.dot_general(a, b, (((1,), (1,)), ((), ())), preferred_element_type=F32)


def tn(a, b):
    return lax.dot_general(a, b, (((0,), (0,)), ((), ())), preferred_element_type=F32)


def sigmoid(x):
    return 1.0 / (1.0 + jnp.exp(-x))


def softplus(x):
    return jnp.maximum(x, 0.0) + jnp.log(1.0 + jnp.exp(-jnp.abs(x)))


def iotas(n, m):
    return lax.broadcasted_iota(jnp.int32, (n, m), 0), lax.broadcasted_iota(jnp.int32, (n, m), 1)


def col(array, lane):
    return array[:, lane : lane + 1]


def head_rows(param_ref, heads, rows):
    lane = lax.broadcasted_iota(jnp.int32, (rows, heads * LANES), 1)
    rate = jnp.zeros((rows, heads * LANES), F32)
    bias = jnp.zeros((rows, heads * LANES), F32)
    for h in range(heads):
        here = lane % heads == h
        rate = jnp.where(here, param_ref[0, h], rate)
        bias = jnp.where(here, param_ref[1, h], bias)
    return rate, bias


def proj_kernel(heads, depth, tok_hbm, w_hbm, sw_hbm, proj_ref, gate_ref, wflat_ref, swt_ref, tok_ref, w_ref, sw_ref, wide, swide, sems):
    parts = 3 * heads
    steps = w_ref.shape[0]
    span = depth * parts
    tok_copy = pltpu.make_async_copy(tok_hbm, tok_ref, sems.at[steps])
    sw_copy = pltpu.make_async_copy(sw_hbm, sw_ref, sems.at[steps + 1])
    copies = [pltpu.make_async_copy(w_hbm.at[pl.ds(i * span, span)], w_ref.at[i], sems.at[i]) for i in range(steps)]
    copies[0].start()
    tok_copy.start()
    for copy in copies[1:]:
        copy.start()
    sw_copy.start()
    for i in range(steps):
        copies[i].wait()
        rows = pl.ds(i * depth, depth)
        wide[i % 2] = w_ref[i].astype(F32)
        for part in range(parts):
            wflat_ref[rows, part * 128 : (part + 1) * 128] = wide[i % 2, pl.ds(part, depth, stride=parts), :].astype(BF)
        if i == 0:
            tok_copy.wait()
        add = nn(tok_ref[:, i * depth : (i + 1) * depth], wflat_ref[rows, :])
        if i == 0:
            proj_ref[...] = add
        else:
            proj_ref[...] += add
    sw_copy.wait()
    swide[...] = jnp.zeros_like(swide)
    for level in range(sw_ref.shape[0]):
        swide[pl.ds(level * heads, heads), :] = sw_ref[level].astype(F32)
    swt = swide[...].astype(BF)
    swt_ref[...] = swt
    gate_ref[...] = nt(tok_ref[...], swt)


def project(tokens, qkv_weight, small_weight):
    rows, width = tokens.shape
    heads = qkv_weight.shape[2]
    extra = small_weight.shape[2]
    parts = 3 * heads
    depth = 512
    steps = width // depth
    return pl.pallas_call(
        functools.partial(proj_kernel, heads, depth),
        in_specs=[pl.BlockSpec(memory_space=pltpu.HBM)] * 3,
        out_specs=[pl.BlockSpec(memory_space=VM)] * 4,
        out_shape=[
            jax.ShapeDtypeStruct((rows, parts * 128), F32),
            jax.ShapeDtypeStruct((rows, heads * LANES), F32),
            jax.ShapeDtypeStruct((width, parts * 128), BF),
            jax.ShapeDtypeStruct((heads * LANES, width), BF),
        ],
        scratch_shapes=[
            VM((rows, width), BF), VM((steps, depth * parts, 128), BF), VM((extra, heads, width), BF),
            VM((2, depth * parts, 128), F32), VM((heads * LANES, width), F32), pltpu.SemaphoreType.DMA((steps + 2,)),
        ],
        compiler_params=pltpu.CompilerParams(vmem_limit_bytes=LIMIT["project"] * 2**20),
        name="project",
    )(tokens, qkv_weight.reshape(width * parts, 128), jnp.transpose(small_weight, (2, 1, 0)))


def unit(values):
    scale = lax.rsqrt(jnp.sum(values * values, -1, keepdims=True) + 1e-06)
    return values * scale, scale


def running_log(gate, rate, n):
    row, lane = iotas(n, n)
    lower = jnp.where(row >= lane, 1.0, 0.0).astype(F32)
    return lax.dot_general(
        lower, -rate * sigmoid(gate), (((1,), (0,)), ((), ())),
        precision=lax.Precision.HIGHEST, preferred_element_type=F32,
    )


def mask_rows(n, masks):
    row, lane = iotas(n, n)
    cross = jnp.bitwise_xor(row, lane)
    for k in range(masks.shape[0]):
        masks[k] = jnp.where(jnp.right_shift(cross, k) == 1, 1.0, 0.0).astype(BF)


def local_kernel(heads, levels, group, param_ref, proj_ref, gate_ref, au_ref, e_ref, lp_ref, t_ref, m_ref,
                 nk_ref, core_ref, qh_ref, clog_ref, masks, low):
    n = proj_ref.shape[0]
    gate = gate_ref[...]
    rate, bias = head_rows(param_ref, heads, n)
    clog = running_log(gate, rate, n)
    clog_ref[...] = clog
    clog_t = clog.T
    beta_all = sigmoid(gate + bias)
    lam_all = softplus(gate)
    mask_rows(n, masks)
    row, lane = iotas(n, n)
    cross = jnp.bitwise_xor(row, lane)
    incl = row >= lane
    strict = row > lane
    half = n // 2
    for first in range(0, heads, group):
        hs = range(first, first + group)
        keep = {}
        tb = {}
        score = {}
        for h in hs:
            q, _ = unit(proj_ref[:, h * 128 : (h + 1) * 128])
            k, _ = unit(proj_ref[:, (heads + h) * 128 : (heads + h + 1) * 128])
            v = proj_ref[:, (2 * heads + h) * 128 : (2 * heads + h + 1) * 128]
            qb, kb = q.astype(BF), k.astype(BF)
            beta = col(beta_all, lane_of(h, levels + 1, heads))
            cc = col(clog, lane_of(h, levels, heads))
            at = lane_of(h, levels, heads)
            end = clog_t[at : at + 1, n - 1 : n]
            crow = clog_t[at : at + 1, :]
            e = jnp.where(incl, jnp.exp(cc - crow), 0.0)
            s = (nt(qb, kb) * e).astype(BF)
            lp = jnp.where(strict, nt(kb, kb) * e, 0.0)
            lo = (lp * beta).astype(BF)
            e_ref[h] = e.astype(BF)
            score[h] = s
            lp_ref[h] = lp.astype(BF)
            low[h % group] = lo
            tb[h] = jnp.where(row == lane, 1.0, 0.0).astype(BF) - lo * masks[0]
            grow = jnp.exp(cc)
            keep[h] = (grow * q, (v * beta).astype(BF), ((beta * grow) * k).astype(BF),
                       (jnp.exp(end - cc) * k).astype(BF), end)
        for level in range(1, masks.shape[0]):
            for h in hs:
                w = nn(low[h % group] * masks[level], tb[h]).astype(BF)
                tb[h] = tb[h] - nn(tb[h], w).astype(BF)
        for h in hs:
            gq, vb, kbg, tk, end = keep[h]
            t_ref[h] = tb[h]
            m = nn(score[h], tb[h])
            mb = m.astype(BF)
            m_ref[h] = mb
            mix = nn(tb[h], jnp.concatenate([vb, kbg], 1)).astype(BF)
            nk_ref[h] = mix
            au = tn(mix, tk)
            r2, l2 = iotas(128, 128)
            au_ref[h, 0:128] = au[0:128].astype(BF)
            au_ref[h, 128:256] = (jnp.where(r2 == l2, jnp.exp(end), 0.0) - au[128:256]).astype(BF)
            lam = jnp.where(cross < 64, col(lam_all, lane_of(h, 0, heads)),
                            jnp.where(cross < 128, col(lam_all, lane_of(h, 1, heads)), col(lam_all, lane_of(h, 2, heads))))
            core_ref[h] = nn((m * lam).astype(BF), vb)
            qh_ref[h] = (gq - nn(mb, kbg)).astype(BF)


def local_forward(head_param, proj, gate, levels):
    rows = proj.shape[0]
    heads = head_param.shape[1]
    group = 4
    square = jax.ShapeDtypeStruct((heads, rows, rows), BF)
    bits = rows.bit_length() - 1
    return pl.pallas_call(
        functools.partial(local_kernel, heads, levels, group),
        in_specs=[pl.BlockSpec(memory_space=pltpu.SMEM), pl.BlockSpec(memory_space=VM), pl.BlockSpec(memory_space=VM)],
        out_specs=[pl.BlockSpec(memory_space=VM)] * 9,
        out_shape=[
            jax.ShapeDtypeStruct((heads, 256, 128), BF),
            square, square, square, square,
            jax.ShapeDtypeStruct((heads, rows, 256), BF),
            jax.ShapeDtypeStruct((heads, rows, 128), F32),
            jax.ShapeDtypeStruct((heads, rows, 128), BF),
            jax.ShapeDtypeStruct((rows, heads * LANES), F32),
        ],
        scratch_shapes=[VM((bits, rows, rows), BF), VM((group, rows, rows), BF)],
        compiler_params=pltpu.CompilerParams(vmem_limit_bytes=LIMIT["local"] * 2**20),
        name="local_forward",
    )(head_param, proj, gate)


def out_kernel(heads, levels, far, near, gate_ref, core_ref, qh_ref, x_ref, gain_ref, gn_ref,
               normed_ref, g_ref, dqh_ref, gx_ref, dlam_ref):
    n = gate_ref.shape[0]
    lam_all = softplus(gate_ref[...])
    lane = lax.broadcasted_iota(jnp.int32, (n, heads * LANES), 1)
    gain = gain_ref[...]
    dlam = jnp.zeros((n, heads * LANES), F32)
    for h in range(heads):
        qh = qh_ref[h]
        x = x_ref[h]
        w = nt(qh, x)
        core = core_ref[h]
        fw = [col(lam_all, lane_of(h, near + j, heads)) for j in range(far)]
        for j in range(far):
            core = core + fw[j] * w[:, j * 128 : (j + 1) * 128]
        rs = lax.rsqrt(jnp.mean(core * core, -1, keepdims=True) + 1e-06)
        unit_core = core * rs
        normed_ref[:, h * 128 : (h + 1) * 128] = (unit_core * gain).astype(BF)
        gy = gn_ref[:, h * 128 : (h + 1) * 128] * gain
        g = rs * (gy - unit_core * jnp.mean(gy * unit_core, -1, keepdims=True))
        g_ref[h] = g.astype(BF)
        fg = jnp.concatenate([(fw[j] * g).astype(BF) for j in range(far)], 1)
        for j in range(far):
            here = jnp.sum(g * w[:, j * 128 : (j + 1) * 128], -1, keepdims=True)
            dlam = jnp.where(lane == lane_of(h, near + j, heads), here, dlam)
        dqh_ref[h] = nn(fg, x).astype(BF)
        gx_ref[h] = tn(fg, qh).astype(BF)
    dlam_ref[...] = dlam


def out_stage(gate, core, qh, x, gain, grad_normed, levels, far, near):
    rows = gate.shape[0]
    heads = core.shape[0]
    return pl.pallas_call(
        functools.partial(out_kernel, heads, levels, far, near),
        in_specs=[pl.BlockSpec(memory_space=VM)] * 6,
        out_specs=[pl.BlockSpec(memory_space=VM)] * 5,
        out_shape=[
            jax.ShapeDtypeStruct((rows, heads * 128), BF),
            jax.ShapeDtypeStruct((heads, rows, 128), BF),
            jax.ShapeDtypeStruct((heads, rows, 128), BF),
            jax.ShapeDtypeStruct((heads, far * 128, 128), BF),
            jax.ShapeDtypeStruct((rows, heads * LANES), F32),
        ],
        compiler_params=pltpu.CompilerParams(vmem_limit_bytes=LIMIT["out"] * 2**20),
        name="out_stage",
    )(gate, core, qh, x, gain, grad_normed)


def back_kernel(heads, levels, group, param_ref, proj_ref, gate_ref, clog_ref, e_ref, lp_ref, t_ref, m_ref,
                nk_ref, g_ref, dqh_ref, dau_ref, dlam_ref, layer_ref, dproj_ref, dgate_ref, out_ref):
    n = proj_ref.shape[0]
    gate = gate_ref[...]
    rate, bias = head_rows(param_ref, heads, n)
    clog = clog_ref[...]
    beta_all = sigmoid(gate + bias)
    sig_all = sigmoid(gate)
    lam_all = softplus(gate)
    row, lane = iotas(n, n)
    cross = jnp.bitwise_xor(row, lane)
    strict = row > lane
    eye = jnp.where(row == lane, 1.0, 0.0).astype(BF)

    def tq(a, b):
        return nn(nt(eye, a).astype(BF), b)

    out_ref[...] = layer_ref[...]
    wide = lax.broadcasted_iota(jnp.int32, (n, heads * LANES), 1)
    dlam = dlam_ref[...]
    source, target = iotas(n, heads * LANES)

    def pick_level(block, h):
        apart = jnp.bitwise_xor(jnp.right_shift(source, 6), block)
        near_level = jnp.where(apart == 0, 0, jnp.where(apart == 1, 1, 2))
        return jnp.where(target == near_level * heads + h, 1.0, 0.0).astype(BF)

    dlog = jnp.zeros((n, heads * LANES), F32)
    dbeta_all = jnp.zeros((n, heads * LANES), F32)
    last = lax.broadcasted_iota(jnp.int32, (n, 1), 0) == n - 1
    out = [None] * (3 * heads)
    for first in range(0, heads, group):
        for h in range(first, first + group):
            q, rq = unit(proj_ref[:, h * 128 : (h + 1) * 128])
            k, rk = unit(proj_ref[:, (heads + h) * 128 : (heads + h + 1) * 128])
            v = proj_ref[:, (2 * heads + h) * 128 : (2 * heads + h + 1) * 128]
            qb, kb = q.astype(BF), k.astype(BF)
            beta = col(beta_all, lane_of(h, levels + 1, heads))
            cc = col(clog, lane_of(h, levels, heads))
            at = lane_of(h, levels, heads)
            end = clog[n - 1 : n, at : at + 1]
            grow = jnp.exp(cc)
            tail = jnp.exp(end - cc)
            vb = (v * beta).astype(BF)
            kbg = ((beta * grow) * k).astype(BF)
            tk = (tail * k).astype(BF)
            g, dqh = g_ref[h], dqh_ref[h]
            mb, tb, mix = m_ref[h], t_ref[h], nk_ref[h]
            m = mb.astype(F32)
            lam = jnp.where(cross < 64, col(lam_all, lane_of(h, 0, heads)),
                            jnp.where(cross < 128, col(lam_all, lane_of(h, 1, heads)), col(lam_all, lane_of(h, 2, heads))))
            dmw = nt(g, vb)
            prod = m * dmw
            pb = prod.astype(BF)
            dlam = dlam + jnp.concatenate(
                [nn(pb[b * 64 : (b + 1) * 64], pick_level(b, h)) for b in range(n // 64)], 0)
            mw = (m * lam).astype(BF)
            dm = (lam * dmw - nt(dqh, kbg)).astype(BF)
            dau = dau_ref[h]
            du, da = dau[0:128], dau[128:256]
            dnv = nt(tk, du)
            dkt = -nt(tk, da)
            dtk = nn(mix[:, 0:128], du) - nn(mix[:, 128:256], da)
            dmix = jnp.concatenate([dnv.astype(BF), dkt.astype(BF)], 1)
            back = tq(tb, dmix)
            dvb2, dkbg2 = back[:, 0:128], back[:, 128:256]
            dst = nt(dm, tb)
            dstb = dst.astype(BF)
            dvb = tq(mw, g) + dvb2
            both = tq(mb, jnp.concatenate([dqh, dstb], 1))
            dkbg = dkbg2 - both[:, 0:128]
            dlow = both[:, 128:] + nt(back.astype(BF), mix)
            dlow = jnp.where(strict, -dlow, 0.0)
            e = e_ref[h].astype(F32)
            dp = (dst * e).astype(BF)
            lp = lp_ref[h].astype(F32)
            dbeta = jnp.sum(dlow * lp, -1, keepdims=True)
            dkk = (dlow * (beta * e)).astype(BF)
            dq1 = nn(dp, kb)
            dk1 = tq(dp, qb)
            dk2 = nn(dkk, kb)
            dk3 = tq(dkk, kb)
            qr, kr = qb.astype(F32), kb.astype(F32)
            dqf, dtf, dkf = dqh.astype(F32), dtk, dkbg
            gq = jnp.sum(dqf * q, -1, keepdims=True)
            kk = jnp.sum(dkf * k, -1, keepdims=True)
            dtail = jnp.sum(dtf * k, -1, keepdims=True) * tail
            dc = jnp.sum(qr * dq1 + kr * (dk2 - dk1 - dk3), -1, keepdims=True)
            dc = dc + grow * (gq + beta * kk) - dtail
            r2, l2 = iotas(128, 128)
            trace = jnp.sum(jnp.where(r2 == l2, da.astype(F32), 0.0), keepdims=True)
            dend = jnp.sum(dtail, keepdims=True) + jnp.exp(end) * trace
            dc = dc + jnp.where(last, dend, 0.0)
            dbeta = dbeta + jnp.sum(dvb * v, -1, keepdims=True) + grow * kk
            dq = dq1 + grow * dqf
            dk = dk1 + dk2 + dk3 + (beta * grow) * dkf + tail * dtf
            dv = beta * dvb
            out[h] = (rq * (dq - q * jnp.sum(q * dq, -1, keepdims=True))).astype(BF)
            out[heads + h] = (rk * (dk - k * jnp.sum(k * dk, -1, keepdims=True))).astype(BF)
            out[2 * heads + h] = dv.astype(BF)
            dlog = jnp.where(wide == lane_of(h, levels, heads), dc, dlog)
            dbeta_all = jnp.where(wide == lane_of(h, levels + 1, heads), dbeta, dbeta_all)
    upper = jnp.where(lane >= row, 1.0, 0.0).astype(F32)
    dstep = lax.dot_general(upper, dlog, (((1,), (0,)), ((), ())),
                            precision=lax.Precision.HIGHEST, preferred_element_type=F32)
    dgate = dlam * sig_all - rate * sig_all * (1.0 - sig_all) * dstep + beta_all * (1.0 - beta_all) * dbeta_all
    dgate_ref[...] = dgate.astype(BF)
    for j, grad in enumerate(out):
        dproj_ref[:, j * 128 : (j + 1) * 128] = grad


def back_stage(head_param, proj, gate, clog, saved, g, dqh, dau, dlam, layer, levels):
    rows = proj.shape[0]
    heads = head_param.shape[1]
    return pl.pallas_call(
        functools.partial(back_kernel, heads, levels, 1),
        in_specs=[pl.BlockSpec(memory_space=pltpu.SMEM)] + [pl.BlockSpec(memory_space=VM)] * 13,
        out_specs=[pl.BlockSpec(memory_space=VM)] * 3,
        out_shape=[jax.ShapeDtypeStruct((rows, 3 * heads * 128), BF), jax.ShapeDtypeStruct((rows, heads * LANES), BF),
                   jax.ShapeDtypeStruct(layer.shape, BF)],
        compiler_params=pltpu.CompilerParams(vmem_limit_bytes=LIMIT["back"] * 2**20),
        name="back_stage",
    )(head_param, proj, gate, clog, *saved, g, dqh, dau, dlam, layer)


MESH = pl.DeviceIdType.MESH
RING = 4


def place():
    ctx = lax.axis_index("ctx")
    return lax.div(ctx, 2 * RING), lax.rem(lax.div(ctx, 2), RING), lax.rem(ctx, 2)


def at_ctx(x, y, core):
    return {"ctx": (x * RING + y) * 2 + core}


def around(index, step):
    return lax.rem(index + step + RING, RING)


def greet(peers):
    barrier = pltpu.get_barrier_semaphore()
    for peer in peers:
        pl.semaphore_signal(barrier, inc=1, device_id=peer, device_id_type=MESH)
    pl.semaphore_wait(barrier, len(peers))


def remote(src, dst, send, recv, index, peer):
    return pltpu.make_async_remote_copy(
        src_ref=src, dst_ref=dst, send_sem=send.at[index], recv_sem=recv.at[index],
        device_id=peer, device_id_type=MESH)


class Ring:
    def __init__(self, buf, i, send, recv, base, right, left, low, middle):
        rows = buf.shape[2]
        first, second, whole = pl.ds(low, middle - low), pl.ds(middle, rows - middle), pl.ds(0, middle)

        def copy(index, slot, to, part, peer):
            return remote(buf.at[slot, i, part], buf.at[to, i, part], send, recv, base + index, peer)

        self.near = [copy(0, 0, 1, first, right), copy(1, 0, 3, second, left),
                     copy(2, 0, 1, second, right), copy(3, 0, 3, whole, left)]
        self.far = [copy(4, 1, 2, first, right), copy(5, 3, 2, second, left)]
        for one in self.near:
            one.start()

    def relay(self):
        for near, far in zip(self.near, self.far):
            near.wait_recv()
            far.start()

    def arrive(self):
        for one in self.near[2:] + self.far:
            one.wait_recv()

    def leave(self):
        for one in self.near + self.far:
            one.wait_send()


def flag(cond):
    return jnp.where(cond, 1.0, 0.0).astype(F32)


def gather_kernel(au_ref, gout_ref, ow_ref, x_ref, cores_ref, ys_ref, xs_ref, gn_ref, cores, ys, xs, share, send, recv, local):
    x, y, core = place()
    partner = at_ctx(x, y, 1 - core)
    y_right, y_left = at_ctx(x, around(y, 1), core), at_ctx(x, around(y, -1), core)
    x_right, x_left = at_ctx(around(x, 1), y, core), at_ctx(around(x, -1), y, core)
    greet((partner, y_right, y_left, x_right, x_left))
    first = core * 2
    mine, yours = pl.ds(first, 2), pl.ds(2 - first, 2)
    out = [remote(au_ref.at[part], cores.at[core, part], send, recv, k, partner) for k, part in enumerate((yours, mine))]
    take = [remote(au_ref.at[part], cores.at[1 - core, part], send, recv, k, partner) for k, part in enumerate((mine, yours))]
    for one in out:
        one.start()
    keep = pltpu.make_async_copy(au_ref, cores.at[core], local.at[0])
    keep.start()
    gn_ref[...] = nt(gout_ref[...], ow_ref[...])
    eye_r, eye_c = iotas(128, 128)
    eye = jnp.where(eye_r == eye_c, 1.0, 0.0).astype(F32)

    def joined(below, above):
        moved = nn(below, above[128:256])
        return jnp.concatenate([moved[0:128] + above[0:128].astype(F32), moved[128:256]], 0)

    keep.wait()
    take[0].wait_recv()
    ring = []
    for i in range(2):
        ys[0, i] = joined(cores[0, first + i], cores[1, first + i]).astype(BF)
        ring.append(Ring(ys, i, send, recv, 2 + 6 * i, y_right, y_left, 0, 128))
    for i in range(2):
        ring[i].relay()
    prefix = [None, None]
    cols = []
    for i in range(2):
        ring[i].arrive()
        at = [ys[around(y, -k), i] for k in range(RING)]
        s1 = joined(at[0], at[1])
        s2 = joined(s1.astype(BF), at[2])
        s3 = joined(s2.astype(BF), at[3])
        xs[0, i] = s3.astype(BF)
        cols.append(Ring(xs, i, send, recv, 14 + 6 * i, x_right, x_left, 0, 128))
        x1 = flag(lax.rem(y, 2) == 1) * ys[1, i, 0:128].astype(F32)
        s1u = s1[0:128]
        x2 = flag(y == 2) * s1u + flag(y == 3) * nn(s1u.astype(BF), at[2][128:256])
        share[first + i, 0:128] = x1.astype(BF)
        share[first + i, 128:256] = x2.astype(BF)
        prefix[i] = (flag(y == 0) * eye + flag(y == 1) * at[0][128:256].astype(F32)
                     + flag(y == 2) * s1[128:256] + flag(y == 3) * s2[128:256]).astype(BF)
    for i in range(2):
        cols[i].relay()
    give, got = [], []
    for i in range(2):
        cols[i].arrive()
        at = [xs[around(x, -k), i] for k in range(RING)]
        r1 = nn(at[0][0:128], at[1][128:256]) + at[1][0:128].astype(F32)
        x3 = flag(lax.rem(x, 2) == 1) * xs[1, i, 0:128].astype(F32)
        x4 = flag(x == 2) * r1 + flag(x == 3) * nn(r1.astype(BF), at[2][128:256])
        both = jnp.concatenate([x3.astype(BF), x4.astype(BF)], 0)
        share[first + i, 256:512] = nn(both, prefix[i]).astype(BF)
        give.append(remote(share.at[first + i], share.at[first + i], send, recv, 26 + i, partner))
        got.append(remote(share.at[2 - first + i], share.at[2 - first + i], send, recv, 26 + i, partner))
        give[i].start()
    upper = flag(core == 1)
    take[1].wait_recv()
    step = []
    for h in range(4):
        below = cores[0, h]
        x_ref[h, 0:128] = (upper * below[0:128].astype(F32)).astype(BF)
        step.append((upper * below[128:256].astype(F32) + (1.0 - upper) * eye).astype(BF))
    cores_ref[...] = cores[...]
    ys_ref[...] = ys[...]
    xs_ref[...] = xs[...]
    for i in range(2):
        x_ref[first + i, 128:640] = nn(share[first + i], jnp.where(core == 0, step[i], step[2 + i])).astype(BF)
    for i in range(2):
        got[i].wait_recv()
        x_ref[2 - first + i, 128:640] = nn(share[2 - first + i], jnp.where(core == 0, step[2 + i], step[i])).astype(BF)
    for one in out + give:
        one.wait_send()
    for one in ring + cols:
        one.leave()


def gather_states(au, grad_out, out_weight):
    heads = au.shape[0]
    cores = ((2, heads, 256, 128), BF)
    ring = ((RING, 2, 256, 128), BF)
    return pl.pallas_call(
        gather_kernel,
        in_specs=[pl.BlockSpec(memory_space=VM)] * 3,
        out_specs=[pl.BlockSpec(memory_space=VM)] * 5,
        out_shape=[jax.ShapeDtypeStruct((heads, 640, 128), BF)] + [jax.ShapeDtypeStruct(*s) for s in (cores, ring, ring)]
        + [jax.ShapeDtypeStruct((grad_out.shape[0], heads * 128), F32)],
        scratch_shapes=[VM(*cores), VM(*ring), VM(*ring), VM((heads, 512, 128), BF),
                        pltpu.SemaphoreType.DMA((28,)), pltpu.SemaphoreType.DMA((28,)), pltpu.SemaphoreType.DMA((1,))],
        compiler_params=pltpu.CompilerParams(
            collective_id=1, has_side_effects=True, vmem_limit_bytes=LIMIT["gather"] * 2**20),
        name="gather_states",
    )(au, grad_out, out_weight)


def return_kernel(groups, gx_ref, x_ref, cores_ref, ys_ref, xs_ref, normed_ref, ow_ref, dau_ref, layer_ref,
                  part_ref, pair, ys, xs, share, chunks, send, recv, local, zsend, zrecv):
    x, y, core = place()
    z = lax.axis_index("head")
    partner = at_ctx(x, y, 1 - core)
    y_right, y_left = at_ctx(x, around(y, 1), core), at_ctx(x, around(y, -1), core)
    x_right, x_left = at_ctx(around(x, 1), y, core), at_ctx(around(x, -1), y, core)
    across = [{"head": lax.rem(z + k, groups)} for k in range(1, groups)]
    greet([partner, y_right, y_left, x_right, x_left] + across)
    first = core * 2
    mine, yours = pl.ds(first, 2), pl.ds(2 - first, 2)
    out = [remote(gx_ref.at[part], pair.at[core, part], send, recv, k, partner) for k, part in enumerate((yours, mine))]
    take = [remote(gx_ref.at[part], pair.at[1 - core, part], send, recv, k, partner) for k, part in enumerate((mine, yours))]
    for one in out:
        one.start()
    keep = pltpu.make_async_copy(gx_ref, pair.at[core], local.at[0])
    keep.start()
    wide = part_ref.shape[2]
    for j in range(groups):
        part_ref[j] = nn(normed_ref[...], ow_ref[:, j * wide : (j + 1) * wide]).astype(BF)
    spread = []
    for k in range(1, groups):
        to = lax.rem(z + k, groups)
        spread.append(remote(part_ref.at[to], chunks.at[k - 1], zsend, zrecv, k - 1, across[k - 1]))
        spread[-1].start()
    upper = flag(core == 1)
    bits = [upper, flag(lax.rem(y, 2) == 1), flag(y >= 2), flag(lax.rem(x, 2) == 1), flag(x >= 2)]
    eye_r, eye_c = iotas(128, 128)
    eye = jnp.where(eye_r == eye_c, 1.0, 0.0).astype(F32)
    after = [None, None]
    for i in range(2):
        at = [ys_ref[around(y, -k), i, 128:256] for k in range(RING)]
        q1 = nn(at[2], at[3])
        q0 = nn(at[1], q1.astype(BF))
        after[i] = (flag(y == 3) * eye + flag(y == 2) * at[3].astype(F32) + flag(y == 1) * q1 + flag(y == 0) * q0).astype(BF)
    keep.wait()
    take[0].wait_recv()
    ring = []
    for i in range(2):
        total = pair[0, first + i, 128:640].astype(F32) + nt(pair[1, first + i, 128:640], cores_ref[0, first + i, 128:256])
        for k in range(4):
            ys[0, i, k * 128 : (k + 1) * 128] = (bits[k + 1] * total[k * 128 : (k + 1) * 128]).astype(BF)
        ring.append(Ring(ys, i, send, recv, 2 + 6 * i, y_right, y_left, 128, 320))
    for i in range(2):
        ring[i].relay()
    held = [None, None]
    cols = []
    for i in range(2):
        ring[i].arrive()
        trans = [ys_ref[around(y, -k), i, 128:256] for k in range(RING)]
        at = [ys[around(y, -k), i, 128:512] for k in range(RING)]
        h1 = nt(at[3], trans[2]) + at[2].astype(F32)
        h0 = nt(h1.astype(BF), trans[1]) + at[1].astype(F32)
        column = nt(h0[128:384].astype(BF), trans[0]) + at[0][128:384].astype(F32)
        xs[0, i] = column.astype(BF)
        cols.append(Ring(xs, i, send, recv, 14 + 6 * i, x_right, x_left, 0, 128))
        held[i] = flag(y == 2) * at[3].astype(F32) + flag(y == 1) * h1 + flag(y == 0) * h0
        share[first + i, 0:128] = ((1.0 - bits[1]) * ys[3, i, 0:128].astype(F32)).astype(BF)
        share[first + i, 128:256] = held[i][0:128].astype(BF)
    for i in range(2):
        cols[i].relay()
    give, got = [], []
    for i in range(2):
        cols[i].arrive()
        trans = [xs_ref[around(x, -k), i, 128:256] for k in range(RING)]
        at = [xs[around(x, -k), i, 128:256] for k in range(RING)]
        h1 = nt(at[3], trans[2]) + at[2].astype(F32)
        h0 = nt(h1.astype(BF), trans[1]) + at[1].astype(F32)
        v4 = flag(x == 2) * at[3].astype(F32) + flag(x == 1) * h1 + flag(x == 0) * h0
        v3 = (1.0 - bits[3]) * xs[3, i, 0:128].astype(F32)
        both = jnp.concatenate([v3.astype(BF), v4.astype(BF)], 0)
        share[first + i, 256:512] = (held[i][128:384] + nt(both, after[i])).astype(BF)
        give.append(remote(share.at[first + i], share.at[first + i], send, recv, 26 + i, partner))
        got.append(remote(share.at[2 - first + i], share.at[2 - first + i], send, recv, 26 + i, partner))
        give[i].start()
    take[1].wait_recv()

    def finish(h):
        move = (upper * eye + (1.0 - upper) * cores_ref[1, h, 128:256].astype(F32)).astype(BF)
        v = nt(share[h], move)
        parts = [(1.0 - upper) * pair[1, h, 0:128].astype(F32)]
        for k in range(4):
            keep_it = (1.0 - upper) * bits[k + 1]
            parts.append(v[k * 128 : (k + 1) * 128] + keep_it * pair[1, h, (k + 1) * 128 : (k + 2) * 128].astype(F32))
        so_far = jnp.zeros((128, 128), F32)
        du = jnp.zeros((128, 128), F32)
        states = []
        for k in range(5):
            state = x_ref[h, k * 128 : (k + 1) * 128].astype(F32)
            states.append((bits[k] * state + (1.0 - bits[k]) * so_far).astype(BF))
            so_far = so_far + state
            du = du + (1.0 - bits[k]) * parts[k]
        da = tn(jnp.concatenate(states, 0), jnp.concatenate([p.astype(BF) for p in parts], 0))
        dau_ref[h, 0:128] = du.astype(BF)
        dau_ref[h, 128:256] = da.astype(BF)

    for i in range(2):
        finish(first + i)
    for i in range(2):
        got[i].wait_recv()
        finish(2 - first + i)
    total = part_ref[z].astype(F32)
    for copy in spread:
        copy.wait_recv()
    for k in range(groups - 1):
        total = total + chunks[k].astype(F32)
    layer_ref[...] = total.astype(BF)
    for one in out + give + spread:
        one.wait_send()
    for one in ring + cols:
        one.leave()


def return_grads(gx, x, cores, ys, xs, normed, out_weight, groups):
    heads = gx.shape[0]
    rows, wide = normed.shape[0], out_weight.shape[1] // groups
    ring = (RING, 2)
    return pl.pallas_call(
        functools.partial(return_kernel, groups),
        in_specs=[pl.BlockSpec(memory_space=VM)] * 7,
        out_specs=[pl.BlockSpec(memory_space=VM)] * 2,
        out_shape=[jax.ShapeDtypeStruct((heads, 256, 128), BF), jax.ShapeDtypeStruct((rows, wide), BF)],
        scratch_shapes=[VM((groups, rows, wide), BF), VM((2, heads, 640, 128), BF), VM(ring + (512, 128), BF), VM(ring + (256, 128), BF),
                        VM((heads, 512, 128), BF), VM((3, rows, wide), BF),
                        pltpu.SemaphoreType.DMA((28,)), pltpu.SemaphoreType.DMA((28,)), pltpu.SemaphoreType.DMA((1,)),
                        pltpu.SemaphoreType.DMA((3,)), pltpu.SemaphoreType.DMA((3,))],
        compiler_params=pltpu.CompilerParams(
            collective_id=2, has_side_effects=True, vmem_limit_bytes=LIMIT["return"] * 2**20),
        name="return_grads",
    )(gx, x, cores, ys, xs, normed, out_weight)


def last_kernel(groups, dproj_ref, dgate_ref, w_ref, sw_ref, out_ref, mine, relay, direct, extra, arrive, send, recv):
    rows, wide = out_ref.shape
    z = lax.axis_index("head")
    half = wide // 2
    right, left = {"head": lax.rem(z + 1, groups)}, {"head": lax.rem(z + groups - 1, groups)}
    greet((right, left))
    dproj, dgate = dproj_ref[...], dgate_ref[...]

    def product(step):
        chunk = lax.rem(z + step + groups, groups)
        at = pl.ds(pl.multiple_of(chunk * wide, wide), wide)
        return nt(dproj, w_ref[at, :]) + nn(dgate, sw_ref[:, at])

    far = product(2)
    relay[0] = far[:, :half].astype(BF)
    relay[1] = far[:, half:].astype(BF)
    far_right = remote(relay.at[0], arrive.at[0], send, recv, 0, right)
    far_left = remote(relay.at[1], arrive.at[1], send, recv, 1, left)
    far_right.start()
    far_left.start()
    to_right = product(1)
    direct[0] = to_right[:, half:].astype(BF)
    near_right = remote(direct.at[0], arrive.at[2], send, recv, 2, right)
    near_right.start()
    to_left = product(-1)
    direct[1] = to_left[:, :half].astype(BF)
    near_left = remote(direct.at[1], arrive.at[3], send, recv, 3, left)
    near_left.start()
    far_right.wait_recv()
    extra[0] = (to_right[:, :half] + arrive[0].astype(F32)).astype(BF)
    sum_right = remote(extra.at[0], arrive.at[4], send, recv, 4, right)
    sum_right.start()
    far_left.wait_recv()
    extra[1] = (to_left[:, half:] + arrive[1].astype(F32)).astype(BF)
    sum_left = remote(extra.at[1], arrive.at[5], send, recv, 5, left)
    sum_left.start()
    mine[...] = product(0)
    near_right.wait_recv()
    near_left.wait_recv()
    sum_right.wait_recv()
    sum_left.wait_recv()
    out_ref[:, :half] = (mine[:, :half] + arrive[4].astype(F32) + arrive[3].astype(F32)).astype(BF)
    out_ref[:, half:] = (mine[:, half:] + arrive[5].astype(F32) + arrive[2].astype(F32)).astype(BF)
    for copy in (far_right, far_left, near_right, near_left, sum_right, sum_left):
        copy.wait_send()


def last_stage(dproj, dgate, wflat, swt, groups):
    rows = dproj.shape[0]
    wide = wflat.shape[0] // groups
    half = (rows, wide // 2)
    return pl.pallas_call(
        functools.partial(last_kernel, groups),
        in_specs=[pl.BlockSpec(memory_space=VM)] * 4,
        out_specs=pl.BlockSpec(memory_space=VM),
        out_shape=jax.ShapeDtypeStruct((rows, wide), BF),
        scratch_shapes=[VM((rows, wide), F32), VM((2,) + half, BF), VM((2,) + half, BF), VM((2,) + half, BF),
                        VM((6,) + half, BF), pltpu.SemaphoreType.DMA((6,)), pltpu.SemaphoreType.DMA((6,))],
        compiler_params=pltpu.CompilerParams(
            collective_id=3, has_side_effects=True, vmem_limit_bytes=LIMIT["last"] * 2**20),
        name="last_stage",
    )(dproj, dgate, wflat, swt)


def on_device(tokens, qkv_weight, small_weight, head_param, norm_gain, out_weight, grad_out):
    rows, width = tokens.shape
    heads = qkv_weight.shape[2]
    levels = small_weight.shape[2] - 2
    near = (rows // 64).bit_length()
    far = lax.axis_size("ctx").bit_length() - 1
    groups = lax.axis_size("head")
    rates = head_param.T
    proj, gate, wflat, swt = project(tokens, qkv_weight, small_weight)
    au, *saved, core, qh, clog = local_forward(rates, proj, gate, levels)
    flat_out = out_weight.reshape(heads * 128, width)
    x, cores, ys, xs, grad_normed = gather_states(au, grad_out, flat_out)
    normed, g, dqh, gx, dlam = out_stage(gate, core, qh, x, norm_gain.reshape(1, -1), grad_normed, levels, far, near)
    dau, layer = return_grads(gx, x, cores, ys, xs, normed, flat_out, groups)
    dproj, dgate, layer_out = back_stage(rates, proj, gate, clog, saved, g, dqh, dau, dlam, layer, levels)
    grad_tokens = last_stage(dproj, dgate, wflat, swt, groups)
    return (layer_out, grad_tokens)


def solution(mesh):
    placed = (
        P("ctx", None),
        P(None, None, "head", None),
        P(None, "head", None),
        P("head", None),
        P(),
        P("head", None, None),
        P("ctx", None),
    )
    return jax.shard_map(
        on_device,
        mesh=mesh,
        in_specs=placed,
        out_specs=(P("ctx", "head"), P("ctx", "head")),
        check_vma=False,
    )
```

time: 123 us -> 89.1 us (0.72)
  Pallas kernels: 114 us -> 85.2 us
  local copies, waits for them, and re-layouts: 7.65 us -> 3.03 us
    pallas_call x2, Pallas kernels: 37.1 us -> 29.2 us  [the longest x1 23.4 us: gather_states(): pl.pallas_call(gather_kernel, in_specs=[pl.BlockSpec(memory_space=VM)] *...]
    pallas_call x1, Pallas kernels: 11 us -> 6.27 us  [local_forward(): pl.pallas_call(functools.partial(local_kernel, heads, levels, group), in_...]
    unnamed x6 -> x13, local copies, waits for them, and re-layouts: 7.65 us -> 3.03 us
    pallas_call x1, Pallas kernels: 30.9 us -> 26.6 us  [return_grads(): pl.pallas_call(functools.partial(return_kernel, groups), in_specs=[pl.Blo...]
    pallas_call x1, Pallas kernels: 11.4 us -> 7.25 us  [back_stage(): pl.pallas_call(functools.partial(back_kernel, heads, levels, 1), in_specs...]
    pallas_call x1, Pallas kernels: 7.31 us -> 3.24 us  [out_stage(): pl.pallas_call(functools.partial(out_kernel, heads, levels, far, near), i...]
    pallas_call x1, Pallas kernels: 16.5 us -> 12.6 us  [last_stage(): pl.pallas_call(functools.partial(last_kernel, groups), in_specs=[pl.Block...]
where the time goes in v3:
time: 89.1 us; the launch traced here: 89 us
  Pallas kernels  85.2 us (96%)
  local copies, waits for them, and re-layouts  3.03 us (3%)
    pallas_call x1, Pallas kernels, return_grads(): pl.pallas_call(functools.partial(return_kernel, groups), in_specs=[pl.Blo...  26.6 us
    pallas_call x1, Pallas kernels, gather_states(): pl.pallas_call(gather_kernel, in_specs=[pl.BlockSpec(memory_space=VM)] *...  23.4 us
    pallas_call x1, Pallas kernels, last_stage(): pl.pallas_call(functools.partial(last_kernel, groups), in_specs=[pl.Block...  12.6 us
    pallas_call x1, Pallas kernels, back_stage(): pl.pallas_call(functools.partial(back_kernel, heads, levels, 1), in_specs...  7.25 us
    pallas_call x1, Pallas kernels, local_forward(): pl.pallas_call(functools.partial(local_kernel, heads, levels, group), in_...  6.27 us
    pallas_call x1, Pallas kernels, project(): pl.pallas_call(functools.partial(proj_kernel, heads, depth), in_specs=[pl...  5.84 us
    pallas_call x1, Pallas kernels, out_stage(): pl.pallas_call(functools.partial(out_kernel, heads, levels, far, near), i...  3.24 us
    unnamed x13, local copies, waits for them, and re-layouts  3.03 us

profile of v3, /device:TPU:1, one launch (start us, length us, event | category | flops | bytes accessed | tf_op | source)
XLA Modules:
  0.0 89.0 jit_solution(18015619988684229488)
XLA Ops:
  0.6 0.0 copy-start.1
  0.6 0.0 copy-start
  0.7 0.0 copy-start.2
  0.7 1.4 %copy-done.2 = bf16[256,2048]{1,0:T(8,128)(2,1)S(1)} copy-done((bf16[256,2048]{1,0:T(8,128)(2,1)S(1)}, bf16[256,2048]{1,0:T(8,128)(2,1)}, u32[]{:S(2)}) %copy-start.2) | copy-done | bytes 1048600
  2.0 0.0 copy-start.3
  2.0 0.9 %copy-done.3 = bf16[2048,4,15]{0,1,2:T(4,128)(2,1)S(1)} copy-done((bf16[2048,4,15]{0,1,2:T(4,128)(2,1)S(1)}, bf16[2048,4,15]{0,1,2:T(4,128)(2,1)}, u32[]{:S(2)}) %copy-start.3) | copy-done | bytes 245784
  3.0 0.0 copy-start.4
  3.0 0.0 copy-start.5
  3.0 5.8 %project.1 = (f32[256,1536]{1,0:T(8,128)S(1)}, f32[256,128]{1,0:T(8,128)S(1)}, bf16[2048,1536]{1,0:T(8,128)(2,1)S(1)}, bf16[128,2048]{1,0:T(8,128)(2,1)S(1)}) custom-call(bf16[256,2048]{1,0:T(8,128)(2,1)S(1)} %copy-done.2, bf16[24576,128]{1,0:T(8,128)(2,1)} %bitcast.11, bf16[15,4,2048]{2,1,0:T(4,128)(2,1)S(1)} %bitcast.7), custom_call_target="tpu_custom_call" | custom-call | tf_op jit(solution)/shard_map/project/pallas_call | solution.py:101
  8.8 0.0 copy-done.4
  8.8 6.3 %local_forward.1 = (bf16[4,256,128]{2,1,0:T(8,128)(2,1)S(1)}, bf16[4,256,256]{2,1,0:T(8,128)(2,1)S(1)}, bf16[4,256,256]{2,1,0:T(8,128)(2,1)S(1)}, bf16[4,256,256...) custom-call(f32[2,4]{1,0:T(2,128)S(1)} %bitcast.8, ...), custom_call_target="tpu_custom_call" | custom-call | tf_op jit(solution)/shard_map/local_forward/pallas_call | solution.py:212
  15.1 0.0 copy-done.1
  15.1 0.0 copy-done
  15.1 23.4 %gather_states.1 = (bf16[4,640,128]{2,1,0:T(8,128)(2,1)S(1)}, bf16[2,4,256,128]{3,2,1,0:T(8,128)(2,1)S(1)}, bf16[4,2,256,128]{3,2,1,0:T(8,128)(2,1)S(1)}, bf16[4...) custom-call(bf16[4,256,128]{2,1,0:T(8,128)(2,1)S(1)} %get-tuple-element.40.au_ref, bf16[256,2048]{1,0:T(8,128)(2,1)S(1)} %copy-done.1, ...), custom_call_target="tpu_custom_call" | custom-call | tf_op jit(solution)/shard_map/gather_states/pallas_call | solution.py:552
  38.5 0.0 copy-done.5
  38.5 3.2 %out_stage.1 = (bf16[256,512]{1,0:T(8,128)(2,1)S(1)}, bf16[4,256,128]{2,1,0:T(8,128)(2,1)S(1)}, bf16[4,256,128]{2,1,0:T(8,128)(2,1)S(1)}, bf16[4,640,128]{2,1,0:T(8,128)(2,1)S(1)}, f32[256,128]{1,0:T(8,128)S(1)}) custom-call(f32[256,128]{1,0:T(8,128)S(1)} %get-tuple-element.31.gate_ref, f32[4,256,128]{2,1,0:T(8,128)S(1)} %get-tuple-element.38.core_ref, ...), custom_call_target="tpu_custom_call" | custom-call | tf_op jit(solution)/shard_map/out_stage/pallas_call | solution.py:263
  41.8 26.6 %return_grads.1 = (bf16[4,256,128]{2,1,0:T(8,128)(2,1)S(1)}, bf16[256,512]{1,0:T(8,128)(2,1)S(1)}) custom-call(bf16[4,640,128]{2,1,0:T(8,128)(2,1)S(1)} %get-tuple-element.45.gx_ref, bf16[4,640,128]{2,1,0:T(8,128)(2,1)S(1)} %get-tuple-element.41.x_ref, bf16[2,4,256,128]{3,2,1,0:T(8,128)(2,1)S(1)} %get-tuple-element.46.cores_ref, ...), custom_call_target="tpu_custom_call" | custom-call | tf_op jit(solution)/shard_map/return_grads/pallas_call | solution.py:683
  68.4 7.2 %back_stage.1 = (bf16[256,1536]{1,0:T(8,128)(2,1)S(1)}, bf16[256,128]{1,0:T(8,128)(2,1)S(1)}, bf16[256,512]{1,0:T(8,128)(2,1)}) custom-call(f32[2,4]{1,0:T(2,128)S(1)} %bitcast.9, f32[256,1536]{1,0:T(8,128)S(1)} %get-tuple-element.30.proj_ref, f32[256,128]{1,0:T(8,128)S(1)} %get-tuple-element.31.gate_ref, f32[256,128]{1,0:T(8,128)S(1)} %get-tuple-element.32.clog_ref, ...), custom_call_target="tpu_custom_call" | custom-call | tf_op jit(solution)/shard_map/back_stage/pallas_call | solution.py:393
  75.6 12.6 %last_stage.1 = bf16[256,512]{1,0:T(8,128)(2,1)S(1)} custom-call(bf16[256,1536]{1,0:T(8,128)(2,1)S(1)} %get-tuple-element.54.dproj_ref, bf16[256,128]{1,0:T(8,128)(2,1)S(1)} %get-tuple-element.55.dgate_ref, bf16[2048,1536]{1,0:T(8,128)(2,1)S(1)} %get-tuple-element.56.w_ref, bf16[128,2048]{1,0:T(8,128)(2,1)S(1)} %get-tuple-element.57.sw_ref), custom_call_target="tpu_custom_call" | custom-call | tf_op jit(solution)/shard_map/last_stage/pallas_call | solution.py:749
  88.3 0.7 copy.10
Async XLA Ops:
  0.6 14.5 %copy-start.1 = (bf16[256,2048]{1,0:T(8,128)(2,1)S(1)}, bf16[256,2048]{1,0:T(8,128)(2,1)}, u32[]{:S(2)}) copy-start(bf16[256,2048]{1,0:T(8,128)(2,1)} %gout_ref.1) | copy-start | bytes 3145732
  0.6 14.5 %copy-start = (bf16[4,128,2048]{2,1,0:T(8,128)(2,1)S(1)}, bf16[4,128,2048]{2,1,0:T(8,128)(2,1)}, u32[]{:S(2)}) copy-start(bf16[4,128,2048]{2,1,0:T(8,128)(2,1)} %param.12) | copy-start | bytes 6291460
  0.7 1.4 %copy-start.2 = (bf16[256,2048]{1,0:T(8,128)(2,1)S(1)}, bf16[256,2048]{1,0:T(8,128)(2,1)}, u32[]{:S(2)}) copy-start(bf16[256,2048]{1,0:T(8,128)(2,1)} %tok_hbm.1) | copy-start | bytes 3145732
  2.0 0.9 %copy-start.3 = (bf16[2048,4,15]{0,1,2:T(4,128)(2,1)S(1)}, bf16[2048,4,15]{0,1,2:T(4,128)(2,1)}, u32[]{:S(2)}) copy-start(bf16[2048,4,15]{0,1,2:T(4,128)(2,1)} %param.9) | copy-start | bytes 737284
  3.0 5.9 %copy-start.4 = (f32[4,2]{0,1:T(2,128)S(1)}, f32[4,2]{0,1:T(2,128)}, u32[]{:S(2)}) copy-start(f32[4,2]{0,1:T(2,128)} %param.10) | copy-start | bytes 100
  3.0 35.5 %copy-start.5 = (f32[128]{0:T(128)S(1)}, f32[128]{0:T(128)}, u32[]{:S(2)}) copy-start(f32[128]{0:T(128)} %param.11) | copy-start | bytes 1540

commit v4 on v3

--- a/solution.py
+++ b/solution.py
@@ -77,11 +77,10 @@
             wflat_ref[rows, part * 128 : (part + 1) * 128] = wide[i % 2, pl.ds(part, depth, stride=parts), :].astype(BF)
         if i == 0:
             tok_copy.wait()
-        add = nn(tok_ref[:, i * depth : (i + 1) * depth], wflat_ref[rows, :])
-        if i == 0:
-            proj_ref[...] = add
-        else:
-            proj_ref[...] += add
+        if i == steps // 2 - 1:
+            proj_ref[...] = nn(tok_ref[:, : (i + 1) * depth], wflat_ref[: (i + 1) * depth, :])
+        if i == steps - 1:
+            proj_ref[...] += nn(tok_ref[:, steps // 2 * depth :], wflat_ref[steps // 2 * depth :, :])
     sw_copy.wait()
     swide[...] = jnp.zeros_like(swide)
     for level in range(sw_ref.shape[0]):
@@ -114,7 +113,8 @@
         ],
         compiler_params=pltpu.CompilerParams(vmem_limit_bytes=LIMIT["project"] * 2**20),
         name="project",
-    )(tokens, qkv_weight.reshape(width * parts, 128), jnp.transpose(small_weight, (2, 1, 0)))
+    )(*(pltpu.with_memory_space_constraint(part, pltpu.HBM) for part in (
+        tokens, qkv_weight.reshape(width * parts, 128), jnp.transpose(small_weight, (2, 1, 0)))))
 
 
 def unit(values):
@@ -148,7 +148,10 @@
     clog_t = clog.T
     beta_all = sigmoid(gate + bias)
     lam_all = softplus(gate)
-    mask_rows(n, masks)
+    half = n // 2
+    mask_rows(half, masks)
+    eye_row, eye_col = iotas(half, half)
+    eye = jnp.where(eye_row == eye_col, 1.0, 0.0).astype(BF)
     row, lane = iotas(n, n)
     cross = jnp.bitwise_xor(row, lane)
     incl = row >= lane
@@ -177,14 +180,25 @@
             score[h] = s
             lp_ref[h] = lp.astype(BF)
             low[h % group] = lo
-            tb[h] = jnp.where(row == lane, 1.0, 0.0).astype(BF) - lo * masks[0]
+            for b in range(2):
+                own = lo[b * half : (b + 1) * half, b * half : (b + 1) * half]
+                tb[h, b] = eye - own * masks[0]
             grow = jnp.exp(cc)
             keep[h] = (grow * q, (v * beta).astype(BF), ((beta * grow) * k).astype(BF),
                        (jnp.exp(end - cc) * k).astype(BF), end)
         for level in range(1, masks.shape[0]):
             for h in hs:
-                w = nn(low[h % group] * masks[level], tb[h]).astype(BF)
-                tb[h] = tb[h] - nn(tb[h], w).astype(BF)
+                for b in range(2):
+                    own = pl.ds(b * half, half)
+                    w = nn(low[h % group, own, own] * masks[level], tb[h, b]).astype(BF)
+                    tb[h, b] = tb[h, b] - nn(tb[h, b], w).astype(BF)
+        for h in hs:
+            w = nn(low[h % group, half:, :half], tb[h, 0]).astype(BF)
+            cross_part = nn(tb[h, 1], w)
+            tb[h] = jnp.concatenate([
+                jnp.concatenate([tb[h, 0], jnp.zeros((half, half), BF)], 1),
+                jnp.concatenate([(-cross_part).astype(BF), tb[h, 1]], 1),
+            ], 0)
         for h in hs:
             gq, vb, kbg, tk, end = keep[h]
             t_ref[h] = tb[h]
@@ -221,7 +235,7 @@
             jax.ShapeDtypeStruct((heads, rows, 128), BF),
             jax.ShapeDtypeStruct((rows, heads * LANES), F32),
         ],
-        scratch_shapes=[VM((bits, rows, rows), BF), VM((group, rows, rows), BF)],
+        scratch_shapes=[VM((bits - 1, rows // 2, rows // 2), BF), VM((group, rows, rows), BF)],
         compiler_params=pltpu.CompilerParams(vmem_limit_bytes=LIMIT["local"] * 2**20),
         name="local_forward",
     )(head_param, proj, gate)
@@ -418,10 +432,11 @@
     return lax.rem(index + step + RING, RING)
 
 
-def greet(peers):
+def greet(peers, meanwhile):
     barrier = pltpu.get_barrier_semaphore()
     for peer in peers:
         pl.semaphore_signal(barrier, inc=1, device_id=peer, device_id_type=MESH)
+    meanwhile()
     pl.semaphore_wait(barrier, len(peers))
 
 
@@ -468,7 +483,11 @@
     partner = at_ctx(x, y, 1 - core)
     y_right, y_left = at_ctx(x, around(y, 1), core), at_ctx(x, around(y, -1), core)
     x_right, x_left = at_ctx(around(x, 1), y, core), at_ctx(around(x, -1), y, core)
-    greet((partner, y_right, y_left, x_right, x_left))
+
+    def product():
+        gn_ref[...] = nt(gout_ref[...], ow_ref[...])
+
+    greet((partner, y_right, y_left, x_right, x_left), product)
     first = core * 2
     mine, yours = pl.ds(first, 2), pl.ds(2 - first, 2)
     out = [remote(au_ref.at[part], cores.at[core, part], send, recv, k, partner) for k, part in enumerate((yours, mine))]
@@ -477,7 +496,6 @@
         one.start()
     keep = pltpu.make_async_copy(au_ref, cores.at[core], local.at[0])
     keep.start()
-    gn_ref[...] = nt(gout_ref[...], ow_ref[...])
     eye_r, eye_c = iotas(128, 128)
     eye = jnp.where(eye_r == eye_c, 1.0, 0.0).astype(F32)
 
@@ -571,7 +589,13 @@
     y_right, y_left = at_ctx(x, around(y, 1), core), at_ctx(x, around(y, -1), core)
     x_right, x_left = at_ctx(around(x, 1), y, core), at_ctx(around(x, -1), y, core)
     across = [{"head": lax.rem(z + k, groups)} for k in range(1, groups)]
-    greet([partner, y_right, y_left, x_right, x_left] + across)
+    wide = part_ref.shape[2]
+
+    def product():
+        for j in range(groups):
+            part_ref[j] = nn(normed_ref[...], ow_ref[:, j * wide : (j + 1) * wide]).astype(BF)
+
+    greet([partner, y_right, y_left, x_right, x_left] + across, product)
     first = core * 2
     mine, yours = pl.ds(first, 2), pl.ds(2 - first, 2)
     out = [remote(gx_ref.at[part], pair.at[core, part], send, recv, k, partner) for k, part in enumerate((yours, mine))]
@@ -580,9 +604,6 @@
         one.start()
     keep = pltpu.make_async_copy(gx_ref, pair.at[core], local.at[0])
     keep.start()
-    wide = part_ref.shape[2]
-    for j in range(groups):
-        part_ref[j] = nn(normed_ref[...], ow_ref[:, j * wide : (j + 1) * wide]).astype(BF)
     spread = []
     for k in range(1, groups):
         to = lax.rem(z + k, groups)
@@ -605,7 +626,7 @@
         total = pair[0, first + i, 128:640].astype(F32) + nt(pair[1, first + i, 128:640], cores_ref[0, first + i, 128:256])
         for k in range(4):
             ys[0, i, k * 128 : (k + 1) * 128] = (bits[k + 1] * total[k * 128 : (k + 1) * 128]).astype(BF)
-        ring.append(Ring(ys, i, send, recv, 2 + 6 * i, y_right, y_left, 128, 320))
+        ring.append(Ring(ys, i, send, recv, 2 + 6 * i, y_right, y_left, 128, 384))
     for i in range(2):
         ring[i].relay()
     held = [None, None]
@@ -661,15 +682,15 @@
 
     for i in range(2):
         finish(first + i)
-    for i in range(2):
-        got[i].wait_recv()
-        finish(2 - first + i)
     total = part_ref[z].astype(F32)
     for copy in spread:
         copy.wait_recv()
     for k in range(groups - 1):
         total = total + chunks[k].astype(F32)
     layer_ref[...] = total.astype(BF)
+    for i in range(2):
+        got[i].wait_recv()
+        finish(2 - first + i)
     for one in out + give + spread:
         one.wait_send()
     for one in ring + cols:
@@ -700,7 +721,6 @@
     z = lax.axis_index("head")
     half = wide // 2
     right, left = {"head": lax.rem(z + 1, groups)}, {"head": lax.rem(z + groups - 1, groups)}
-    greet((right, left))
     dproj, dgate = dproj_ref[...], dgate_ref[...]
 
     def product(step):
@@ -708,9 +728,12 @@
         at = pl.ds(pl.multiple_of(chunk * wide, wide), wide)
         return nt(dproj, w_ref[at, :]) + nn(dgate, sw_ref[:, at])
 
-    far = product(2)
-    relay[0] = far[:, :half].astype(BF)
-    relay[1] = far[:, half:].astype(BF)
+    def farthest():
+        far = product(2)
+        relay[0] = far[:, :half].astype(BF)
+        relay[1] = far[:, half:].astype(BF)
+
+    greet((right, left), farthest)
     far_right = remote(relay.at[0], arrive.at[0], send, recv, 0, right)
     far_left = remote(relay.at[1], arrive.at[1], send, recv, 1, left)
     far_right.start()

time: 89.1 us -> 85.2 us (0.956)
  local copies, waits for them, and re-layouts: 3.03 us -> 0.72 us
  Pallas kernels: 85.2 us -> 83.6 us
    unnamed x13 -> x9, local copies, waits for them, and re-layouts: 3.03 us -> 0.72 us
where the time goes in v4:
time: 85.2 us; the launch traced here: 85.1 us
  Pallas kernels  83.6 us (98%)
    pallas_call x1, Pallas kernels, return_grads(): pl.pallas_call(functools.partial(return_kernel, groups), in_specs=[pl.Blo...  26.7 us
    pallas_call x1, Pallas kernels, gather_states(): pl.pallas_call(gather_kernel, in_specs=[pl.BlockSpec(memory_space=VM)] *...  22.9 us
    pallas_call x1, Pallas kernels, last_stage(): pl.pallas_call(functools.partial(last_kernel, groups), in_specs=[pl.Block...  11.9 us
    pallas_call x1, Pallas kernels, back_stage(): pl.pallas_call(functools.partial(back_kernel, heads, levels, 1), in_specs...  7.24 us
    pallas_call x1, Pallas kernels, project(): pl.pallas_call(functools.partial(proj_kernel, heads, depth), in_specs=[pl...  6.21 us
    pallas_call x1, Pallas kernels, local_forward(): pl.pallas_call(functools.partial(local_kernel, heads, levels, group), in_...  5.4 us
    pallas_call x1, Pallas kernels, out_stage(): pl.pallas_call(functools.partial(out_kernel, heads, levels, far, near), i...  3.24 us

profile of v4, /device:TPU:1, one launch (start us, length us, event | category | flops | bytes accessed | tf_op | source)
XLA Modules:
  0.0 85.1 jit_solution(2839592784912840957)
XLA Ops:
  0.6 0.0 copy-start.1
  0.6 0.0 copy-start
  0.7 0.0 copy-start.2
  0.7 0.0 copy-start.3
  0.7 6.2 %project.1 = (f32[256,1536]{1,0:T(8,128)S(1)}, f32[256,128]{1,0:T(8,128)S(1)}, bf16[2048,1536]{1,0:T(8,128)(2,1)S(1)}, bf16[128,2048]{1,0:T(8,128)(2,1)S(1)}) custom-call(bf16[256,2048]{1,0:T(8,128)(2,1)} %tok_hbm.1, bf16[24576,128]{1,0:T(8,128)(2,1)} %bitcast.10, bf16[15,4,2048]{2,1,0:T(4,128)(2,1)} %bitcast.11), custom_call_target="tpu_custom_call" | custom-call | tf_op jit(solution)/shard_map/project/pallas_call | solution.py:100
  6.9 0.0 copy-done.2
  6.9 5.4 %local_forward.1 = (bf16[4,256,128]{2,1,0:T(8,128)(2,1)S(1)}, bf16[4,256,256]{2,1,0:T(8,128)(2,1)S(1)}, bf16[4,256,256]{2,1,0:T(8,128)(2,1)S(1)}, bf16[4,256,256...) custom-call(f32[2,4]{1,0:T(2,128)S(1)} %bitcast.7, ...), custom_call_target="tpu_custom_call" | custom-call | tf_op jit(solution)/shard_map/local_forward/pallas_call | solution.py:226
  12.3 0.0 copy-done.1
  12.3 0.0 copy-done
  12.3 22.9 %gather_states.1 = (bf16[4,640,128]{2,1,0:T(8,128)(2,1)S(1)}, bf16[2,4,256,128]{3,2,1,0:T(8,128)(2,1)S(1)}, bf16[4,2,256,128]{3,2,1,0:T(8,128)(2,1)S(1)}, bf16[4...) custom-call(bf16[4,256,128]{2,1,0:T(8,128)(2,1)S(1)} %get-tuple-element.40.au_ref, bf16[256,2048]{1,0:T(8,128)(2,1)S(1)} %copy-done.1, ...), custom_call_target="tpu_custom_call" | custom-call | tf_op jit(solution)/shard_map/gather_states/pallas_call | solution.py:570
  35.2 0.0 copy-done.3
  35.2 3.2 %out_stage.1 = (bf16[256,512]{1,0:T(8,128)(2,1)S(1)}, bf16[4,256,128]{2,1,0:T(8,128)(2,1)S(1)}, bf16[4,256,128]{2,1,0:T(8,128)(2,1)S(1)}, bf16[4,640,128]{2,1,0:T(8,128)(2,1)S(1)}, f32[256,128]{1,0:T(8,128)S(1)}) custom-call(f32[256,128]{1,0:T(8,128)S(1)} %get-tuple-element.31.gate_ref, f32[4,256,128]{2,1,0:T(8,128)S(1)} %get-tuple-element.38.core_ref, ...), custom_call_target="tpu_custom_call" | custom-call | tf_op jit(solution)/shard_map/out_stage/pallas_call | solution.py:277
  38.4 26.7 %return_grads.1 = (bf16[4,256,128]{2,1,0:T(8,128)(2,1)S(1)}, bf16[256,512]{1,0:T(8,128)(2,1)S(1)}) custom-call(bf16[4,640,128]{2,1,0:T(8,128)(2,1)S(1)} %get-tuple-element.45.gx_ref, bf16[4,640,128]{2,1,0:T(8,128)(2,1)S(1)} %get-tuple-element.41.x_ref, bf16[2,4,256,128]{3,2,1,0:T(8,128)(2,1)S(1)} %get-tuple-element.46.cores_ref, ...), custom_call_target="tpu_custom_call" | custom-call | tf_op jit(solution)/shard_map/return_grads/pallas_call | solution.py:704
  65.2 7.2 %back_stage.1 = (bf16[256,1536]{1,0:T(8,128)(2,1)S(1)}, bf16[256,128]{1,0:T(8,128)(2,1)S(1)}, bf16[256,512]{1,0:T(8,128)(2,1)}) custom-call(f32[2,4]{1,0:T(2,128)S(1)} %bitcast.8, f32[256,1536]{1,0:T(8,128)S(1)} %get-tuple-element.30.proj_ref, f32[256,128]{1,0:T(8,128)S(1)} %get-tuple-element.31.gate_ref, f32[256,128]{1,0:T(8,128)S(1)} %get-tuple-element.32.clog_ref, ...), custom_call_target="tpu_custom_call" | custom-call | tf_op jit(solution)/shard_map/back_stage/pallas_call | solution.py:407
  72.4 11.9 %last_stage.1 = bf16[256,512]{1,0:T(8,128)(2,1)S(1)} custom-call(bf16[256,1536]{1,0:T(8,128)(2,1)S(1)} %get-tuple-element.54.dproj_ref, bf16[256,128]{1,0:T(8,128)(2,1)S(1)} %get-tuple-element.55.dgate_ref, bf16[2048,1536]{1,0:T(8,128)(2,1)S(1)} %get-tuple-element.56.w_ref, bf16[128,2048]{1,0:T(8,128)(2,1)S(1)} %get-tuple-element.57.sw_ref), custom_call_target="tpu_custom_call" | custom-call | tf_op jit(solution)/shard_map/last_stage/pallas_call | solution.py:772
  84.4 0.7 copy.10
Async XLA Ops:
  0.6 11.7 %copy-start.1 = (bf16[256,2048]{1,0:T(8,128)(2,1)S(1)}, bf16[256,2048]{1,0:T(8,128)(2,1)}, u32[]{:S(2)}) copy-start(bf16[256,2048]{1,0:T(8,128)(2,1)} %gout_ref.1) | copy-start | bytes 3145732
  0.6 11.7 %copy-start = (bf16[4,128,2048]{2,1,0:T(8,128)(2,1)S(1)}, bf16[4,128,2048]{2,1,0:T(8,128)(2,1)}, u32[]{:S(2)}) copy-start(bf16[4,128,2048]{2,1,0:T(8,128)(2,1)} %param.12) | copy-start | bytes 6291460
  0.7 6.2 %copy-start.2 = (f32[4,2]{0,1:T(2,128)S(1)}, f32[4,2]{0,1:T(2,128)}, u32[]{:S(2)}) copy-start(f32[4,2]{0,1:T(2,128)} %param.10) | copy-start | bytes 100
  0.7 34.5 %copy-start.3 = (f32[128]{0:T(128)S(1)}, f32[128]{0:T(128)}, u32[]{:S(2)}) copy-start(f32[128]{0:T(128)} %param.11) | copy-start | bytes 1540
